TPU v7x, 256 devices: a whole 4x4x8 slice. The times are simulated.
256 devices in a mesh: snap: 8 (over x, core), slab: 32 (over y, z).
Axes of the slice: x: 4, y: 4, z: 8, core: 2. Of those that a mesh axis runs over, the one named last changes fastest.
Arguments:
- velocity: bfloat16 [256, 3, 160, 8, 128], P('snap', None, 'slab'), may hold values from -10 to 10
Outputs:
- modes: bfloat16 [768, 32, 5120], P(None, 'slab', 'snap')
- factor: float32 [768, 768], replicated
All inputs are finite; a program needn't handle non-finite values.
Results may differ from a plain program's by a relative error of at most 0.0004.
The roundings to bfloat16 on the way count: a program that leaves them out, or rounds other values in their place, can miss the bound.
Values may be sent and summed in bfloat16 or wider, within the bound.
No kernel may reach another device: no remote copies, remote signals or barrier semaphores. Data moves between devices by JAX's collectives and lax.ppermute only.
A program may use at most 64 MiB of HBM per device.

v0:
```python
import jax
import jax.numpy as jnp
from jax import lax
from jax.experimental import pallas as pl
from jax.experimental.pallas import tpu as pltpu
from jax.sharding import Mesh, PartitionSpec as P

weights = (4.0 / 5.0, -1.0 / 5.0, 4.0 / 105.0, -1.0 / 280.0)
POINTS = 163840
NB = 6
S = 128
F32 = jnp.float32
BF16 = jnp.bfloat16
VM = pl.BlockSpec(memory_space=pltpu.VMEM)


def ramp(field, axis, coeffs):
    total = None
    for shift, coeff in coeffs:
        term = coeff * pltpu.roll(field, shift, axis)
        total = term if total is None else total + term
    return total


def tables():
    shape = (5, 8, 128)
    y = lax.broadcasted_iota(jnp.int32, shape, 1)
    z = lax.broadcasted_iota(jnp.int32, shape, 2)
    ycs = []
    for r in range(1, 8):
        up = jnp.where(y + r < 8, weights[r - 1] if r <= 4 else 0.0, 0.0)
        down = jnp.where(y + r >= 8, weights[7 - r] if r >= 4 else 0.0, 0.0)
        ycs.append((8 - r, (up - down).astype(F32)))
    zcs = []
    for k in range(1, 5):
        zcs.append((128 - k, jnp.where(z + k < 128, weights[k - 1], 0.0).astype(F32)))
        zcs.append((k, jnp.where(z >= k, -weights[k - 1], 0.0).astype(F32)))
    return ycs, zcs


def along_x(parts):
    planes = jnp.concatenate(parts, axis=0)
    total = None
    for k in range(1, 5):
        term = weights[k - 1] * (planes[4 + k : 9 + k] - planes[4 - k : 9 - k])
        total = term if total is None else total + term
    return total


def emit(buf, out, rows):
    for p in range(40):
        out[p // 5, :, (p % 5) * 128 : (p % 5 + 1) * 128] = buf[pl.ds(p, rows, stride=40), :].astype(BF16)


def place(buf, row, value):
    buf[pl.ds(pl.multiple_of(row * 40, 8), 40), :] = value.reshape(40, 128)


def inner_kernel(vel, out, rest, buf):
    ycs, zcs = tables()

    def one(s, carry):
        u = vel[s, 0].astype(F32)
        v = vel[s, 1].astype(F32)
        w = vel[s, 2].astype(F32)
        place(buf, s, ramp(w, 1, ycs) - ramp(v, 2, zcs))
        rest[0, s] = ramp(u, 2, zcs)
        rest[1, s] = ramp(u, 1, ycs)
        return carry

    lax.fori_loop(0, 32, one, 0)
    emit(buf, out, 32)


def outer_kernel(vel, lo, hi, rest, out, buf):
    def one(s, carry):
        v = vel[s, 1].astype(F32)
        w = vel[s, 2].astype(F32)
        dxv = along_x([lo[s, 0].astype(F32), v, hi[s, 0].astype(F32)])
        dxw = along_x([lo[s, 1].astype(F32), w, hi[s, 1].astype(F32)])
        place(buf, s, rest[0, s] - dxw)
        place(buf, 32 + s, dxv - rest[1, s])
        return carry

    lax.fori_loop(0, 32, one, 0)
    emit(buf, out, 64)


def inner(vel):
    return pl.pallas_call(
        inner_kernel,
        out_shape=(jax.ShapeDtypeStruct((8, 32, 640), BF16), jax.ShapeDtypeStruct((2, 32, 5, 8, 128), F32)),
        in_specs=[VM],
        out_specs=(VM, VM),
        scratch_shapes=[pltpu.VMEM((32 * 40, 128), F32)],
        compiler_params=pltpu.CompilerParams(vmem_limit_bytes=16 << 20),
        cost_estimate=pl.CostEstimate(flops=10_000_000, bytes_accessed=12_000_000, transcendentals=0),
    )(vel)


def outer(vel, lo, hi, rest):
    return pl.pallas_call(
        outer_kernel,
        out_shape=jax.ShapeDtypeStruct((8, 64, 640), BF16),
        in_specs=[VM] * 4,
        out_specs=VM,
        scratch_shapes=[pltpu.VMEM((64 * 40, 128), F32)],
        compiler_params=pltpu.CompilerParams(vmem_limit_bytes=16 << 20),
        cost_estimate=pl.CostEstimate(flops=10_000_000, bytes_accessed=6_000_000, transcendentals=0),
    )(vel, lo, hi, rest)


def block(K, J):
    return K * NB - K * (K - 1) // 2 + (J - K)


def gram_kernel(one, two, m, out, buf):
    for j in range(5):
        cols = slice(j * 128, j * 128 + 128)
        for d in range(8):
            buf[j, pl.ds(96 * d, 32, stride=3), :] = one[d, :, cols].astype(F32)
            buf[j, pl.ds(96 * d + 1, 32, stride=3), :] = two[d, 0:32, cols].astype(F32)
            buf[j, pl.ds(96 * d + 2, 32, stride=3), :] = two[d, 32:64, cols].astype(F32)
        m[:, cols] = buf[j].astype(BF16)
    for K in range(NB):
        rows = m[K * S : K * S + S, :]
        res = lax.dot_general(rows, m[K * S :, :], (((1,), (1,)), ((), ())), preferred_element_type=F32)
        for J in range(K, NB):
            b = block(K, J)
            out[b * S : b * S + S, :] = res[:, (J - K) * S : (J - K + 1) * S]
    out[21 * S :, :] = jnp.zeros((S, S), F32)


def gram_blocks(one, two):
    return pl.pallas_call(
        gram_kernel,
        out_shape=(jax.ShapeDtypeStruct((NB * S, 640), BF16), jax.ShapeDtypeStruct((22 * S, S), F32)),
        in_specs=[VM, VM],
        out_specs=(VM, VM),
        scratch_shapes=[pltpu.VMEM((5, NB * S, 128), F32)],
        compiler_params=pltpu.CompilerParams(vmem_limit_bytes=32 << 20),
    )(one, two)


SWAP = [(0, 1), (1, 0)]


def scatter_core(v):
    i = lax.axis_index("c")
    h = v.shape[0] // 2
    send = lax.dynamic_slice_in_dim(v, (1 - i) * h, h, 0)
    keep = lax.dynamic_slice_in_dim(v, i * h, h, 0)
    return keep + lax.ppermute(send, "c", SWAP)


def gather_core(v):
    i = lax.axis_index("c")
    o = lax.ppermute(v, "c", SWAP)
    return jnp.concatenate([jnp.where(i == 0, v, o), jnp.where(i == 0, o, v)], 0)


def ring(n, k):
    return [(j, (j + k) % n) for j in range(n)]


def scatter_x(v):
    i = lax.axis_index("x")
    h = v.shape[0] // 4
    total = lax.dynamic_slice_in_dim(v, i * h, h, 0)
    got = []
    for k in (2, 1, 3):
        send = lax.dynamic_slice_in_dim(v, ((i + k) % 4) * h, h, 0)
        got.append(lax.ppermute(send, "x", ring(4, k)))
    for g in got:
        total = total + g
    return total


def gather_x(v):
    i = lax.axis_index("x")
    h = v.shape[0]
    parts = {0: v}
    for k in (2, 1, 3):
        parts[k] = lax.ppermute(v, "x", ring(4, k))
    out = jnp.zeros((4 * h,) + v.shape[1:], v.dtype)
    for k in range(4):
        out = lax.dynamic_update_slice_in_dim(out, parts[k], ((i - k) % 4) * h, 0)
    return out


def scatter_yz(v):
    got = lax.all_to_all(v.reshape(32, -1, v.shape[1]), ("y", "z"), 0, 0, tiled=True)
    return got.sum(0)


def gather_yz(v):
    got = lax.all_to_all(jnp.broadcast_to(v[None], (32,) + v.shape), ("y", "z"), 0, 0, tiled=True)
    return got.reshape(-1, v.shape[1])


def total_of(v):
    share = scatter_yz(scatter_x(scatter_core(v))) / POINTS
    return gather_core(gather_x(gather_yz(share)))


BF=jnp.bfloat16
def parts(x):
    a=x.astype(BF); r=x-a.astype(jnp.float32)
    b=r.astype(BF); r=r-b.astype(jnp.float32)
    return a,b,r.astype(BF)
def left(p): a,b,c=p; return jnp.concatenate([a,a,b,a,b,c],axis=1)
def right(p): a,b,c=p; return jnp.concatenate([a,b,a,c,b,a],axis=0)
def mm(l,r): return lax.dot_general(l,r,(((1,),(0,)),((),())),preferred_element_type=jnp.float32)

def bi(K,J): return K*NB-K*(K-1)//2+(J-K)
def lane(v,i): return jnp.broadcast_to(v[:,i:i+1],(8,128))
def sub(v,i): return jnp.broadcast_to(v[i:i+1,:],(8,128))
NV=4
def diag(D,T,ones,fill):
    rows=lax.broadcasted_iota(jnp.int32,(8,128),0)
    lanes=lax.broadcasted_iota(jnp.int32,(8,128),1)
    one=ones[...]
    for g in range(16):
        T[8*g:8*g+8,:]=(rows+8*g==lanes).astype(jnp.float32)
    total=len(fill)
    for g in range(16):
        while fill and total-len(fill)<total*(g+1)//15:
            fill.pop(0)()
        Dg=D[8*g:8*g+8,:]; Wg=T[8*g:8*g+8,:]
        B=[lane(Dg,8*g+m)*one for m in range(8)]
        d={(i,m):sub(B[m],i) for m in range(8) for i in range(m,8)}
        inv=[None]*8; F=[None]*8
        dm={}
        for s in range(8):
            inv[s]=1.0/d[s,s]
            for i in range(s+1,8): dm[i,s]=d[i,s]
            F[s]=jnp.where(rows>s,B[s]*inv[s],0.0)
            for m in range(s+1,8):
                B[m]=B[m]-F[s]*d[m,s]
                for i in range(m,8):
                    d[i,m]=d[i,m]-(d[i,s]*d[m,s])*inv[s]
        piv=d[7,7]
        for s in range(7): piv=jnp.where(rows==s,d[s,s],piv)
        rsq=lax.rsqrt(piv)
        U=[];V=[]
        for s in range(8):
            u=sub(Dg,s); v=sub(Wg,s); U.append(u); V.append(v)
            Dg=Dg-F[s]*u; Wg=Wg-F[s]*v
        Rg=jnp.where(lanes>=rows+8*g,Dg*rsq,0.0); Tg=Wg*rsq
        D[8*g:8*g+8,:]=Rg
        T[8*g:8*g+8,:]=Tg
        for h in range(g+1,min(g+1+NV,16)):
            Dh=D[8*h:8*h+8,:]; Wh=T[8*h:8*h+8,:]
            Bh=[lane(Dh,8*g+m) for m in range(8)]
            for s in range(8):
                f=Bh[s]*inv[s]
                for m in range(s+1,8): Bh[m]=Bh[m]-f*dm[m,s]
                Dh=Dh-f*U[s]; Wh=Wh-f*V[s]
            D[8*h:8*h+8,:]=Dh; T[8*h:8*h+8,:]=Wh
        r0=8*(g+1+NV)
        if r0<128:
            p=[q.astype(jnp.float32) for q in parts(jnp.concatenate([Rg,Tg],axis=1))]
            rr=jnp.concatenate([p[0],p[1],p[0],p[2],p[1],p[0]],axis=0).astype(BF)
            ll=jnp.concatenate([p[i][:,:128] for i in (0,0,1,0,1,2)],axis=0)
            upd=mm(jnp.transpose(ll)[r0:,:].astype(BF),rr)
            D[r0:,:]=D[r0:,:]-upd[:,:128]
            T[r0:,:]=T[r0:,:]-upd[:,128:]
def kernel(a_ref,m_ref,ones,f_ref,x_ref,A,T,M,TP,RT,RP,XP):
    n=m_ref.shape[1]
    def zero():
        for K in range(NB):
            if K: f_ref[K*S:K*S+S,0:K*S]=jnp.zeros((S,K*S),jnp.float32)
    fill=[]
    def put(ref,p):
        for i in range(3): ref[i]=p[i]
    def get(ref): return ref[0],ref[1],ref[2]
    for K in range(NB):
        Dk=A.at[bi(K,K)]
        if K==0:
            Dk[...]=a_ref[0]
        diag(Dk,T,ones,fill)
        assert not fill
        f_ref[K*S:K*S+S,K*S:K*S+S]=Dk[...]
        put(TP,parts(T[...]))
        src=a_ref if K==0 else A
        def panel(J,K=K,src=src):
            r=mm(left(get(TP)),right(parts(src[bi(K,J)])))
            f_ref[K*S:K*S+S,J*S:J*S+S]=r
            put(RT.at[J],parts(jnp.transpose(r))); put(RP.at[J],parts(r))
        def update(I,J,K=K,src=src):
            b=bi(I,J)
            A[b]=src[b]-mm(left(get(RT.at[I])),right(get(RP.at[J])))
        def solve(K=K):
            tp=get(TP)
            if K==0:
                m=m_ref[K*S:K*S+S,:]
                xk=mm(jnp.concatenate(tp,axis=1),jnp.concatenate([m,m,m],axis=0))
            else:
                xk=mm(left(tp),right(parts(M[K*S:K*S+S,:])))
            x_ref[K*S:K*S+S,:]=xk.astype(BF)
            if K<NB-1: put(XP,parts(xk))
        def updm(I,K=K):
            m0=m_ref[I*S:I*S+S,:].astype(jnp.float32) if K==0 else M[I*S:I*S+S,:]
            M[I*S:I*S+S,:]=m0-mm(left(get(RT.at[I])),right(get(XP)))
        if K==NB-1:
            solve(); break
        panel(K+1)
        update(K+1,K+1)
        if K==0: fill.append(zero)
        for J in range(K+2,NB): fill.append(lambda J=J,f=panel: f(J))
        fill.append(solve)
        for I in range(K+1,NB):
            for J in range(I,NB):
                if J>K+1: fill.append(lambda I=I,J=J,f=update: f(I,J))
            fill.append(lambda I=I,f=updm: f(I))
def chol_solve(blocks,m):
    n=m.shape[1]
    vm=pl.BlockSpec(memory_space=pltpu.VMEM)
    return pl.pallas_call(kernel,out_shape=(jax.ShapeDtypeStruct((768,768),jnp.float32),jax.ShapeDtypeStruct((768,n),jnp.bfloat16)),
        in_specs=[vm,vm,vm],out_specs=(vm,vm),
        scratch_shapes=[pltpu.VMEM((21,S,S),jnp.float32),pltpu.VMEM((S,S),jnp.float32),pltpu.VMEM((768,n),jnp.float32),pltpu.VMEM((3,S,S),BF),pltpu.VMEM((NB,3,S,S),BF),pltpu.VMEM((NB,3,S,S),BF),pltpu.VMEM((3,S,n),BF)],
        compiler_params=pltpu.CompilerParams(vmem_limit_bytes=40<<20))(blocks,m,jnp.ones((8,128),jnp.float32))


def body(velocity):
    slabs = 32
    forward = [(i, i + 1) for i in range(slabs - 1)]
    backward = [(i + 1, i) for i in range(slabs - 1)]
    lo = lax.ppermute(velocity[:, 1:, 1:5], ("y", "z"), forward)
    hi = lax.ppermute(velocity[:, 1:, 0:4], ("y", "z"), backward)
    share, rest = inner(velocity)
    one = lax.all_to_all(share, ("x", "c"), 0, 0, tiled=True)
    two = lax.all_to_all(outer(velocity, lo, hi, rest), ("x", "c"), 0, 0, tiled=True)
    matrix, blocks = gram_blocks(one, two)
    total = total_of(blocks).reshape(22, S, S)
    factor, modes = chol_solve(total, matrix)
    return modes.reshape(NB * S, 1, 640), factor


def solution(mesh):
    fine = Mesh(mesh.devices.reshape(4, 2, 4, 8), ("x", "c", "y", "z"))
    in_specs = (P(("x", "c"), None, ("y", "z"), None, None),)
    out_specs = (P(None, ("y", "z"), ("x", "c")), P())
    return jax.shard_map(body, mesh=fine, in_specs=in_specs, out_specs=out_specs, check_vma=False)
```

profile of v0, /device:TPU:1, one launch (start us, length us, event | category | flops | bytes accessed | tf_op | source)
XLA Modules:
  0.0 136.9 jit_solution(11962738688515649020)
XLA Ops:
  0.6 0.0 copy-start
  0.6 2.3 %fusion = (bf16[32,2,4,8,128]{4,3,2,1,0:T(8,128)(2,1)}, bf16[32,2,4,8,128]{4,3,2,1,0:T(8,128)(2,1)}) fusion(bf16[32,3,5,8,128]{4,3,2,1,0:T(8,128)(2,1)} %vel.3), kind=kLoop, calls=%fused_computation.14 | loop fusion | bytes 2097152 | tf_op jit(solution)/shard_map/slice | solution.py:330
  3.0 1.3 collective-permute-start.1
  4.3 5.8 %collective-permute-start = (bf16[32,2,4,8,128]{4,3,2,1,0:T(8,128)(2,1)}, bf16[32,2,4,8,128]{4,3,2,1,0:T(8,128)(2,1)}, u32[]{:S(2)}, u32[]{:S(2)}) collective-permute-start(bf16[32,2,4,8,128]{4,3,2,1,0:T(8,128)(2,1)} %get-tuple-element.17), channel_id=1, source_target_pairs={{0,1},{1,2},{2,3},{3,4},{4,5},{5,6},{6,7},{7,8},{8,9},{9,10},{10,1... | collective-permute-start | bytes 1572872 | tf_op jit(solution)/shard_map/ppermute | solution.py:329
  10.0 0.0 copy-done
  10.0 4.5 %shard_map.30 = (bf16[8,32,640]{2,1,0:T(8,128)(2,1)}, f32[2,32,5,8,128]{4,3,2,1,0:T(8,128)S(1)}) custom-call(bf16[32,3,5,8,128]{4,3,2,1,0:T(8,128)(2,1)S(1)} %copy-done), custom_call_target="tpu_custom_call" | custom-call | flops 10000000 | bytes 12000000 | tf_op jit(solution)/shard_map/pallas_call | solution.py:90
  14.6 6.1 %all-to-all-start = ((bf16[8,32,640]{2,1,0:T(8,128)(2,1)}), bf16[8,32,640]{2,1,0:T(8,128)(2,1)S(1)}, u32[]{:S(2)}, u32[]{:S(2)}) async-start(bf16[8,32,640]{2,1,0:T(8,128)(2,1)} %get-tuple-element.8), calls=%async_computation | async-start | bytes 655360 | tf_op jit(solution)/shard_map/all_to_all | solution.py:332
  20.6 0.0 collective-permute-done.1.hi
  20.6 0.0 collective-permute-done.lo
  20.7 3.0 %shard_map.31 = bf16[8,64,640]{2,1,0:T(8,128)(2,1)} custom-call(bf16[32,3,5,8,128]{4,3,2,1,0:T(8,128)(2,1)S(1)} %copy-done, bf16[32,2,4,8,128]{4,3,2,1,0:T(8,128)(2,1)} %collective-permute-done.lo, bf16[32,2,4,8,128]{4,3,2,1,0:T(8,128)(2,1)S(1)} %collective-permute-done.1.hi, f32[2,32,5,8,128]{4,3,2,1,0:T(8,128)S(1)} %get-tuple-element.9.rest), custom_call_target="tpu_custom_call" | custom-call | flops 10000000 | bytes 6000000 | tf_op jit(solution)/shard_map/pallas_call | solution.py:102
  23.6 4.1 %all-to-all-done.one = bf16[8,32,640]{2,1,0:T(8,128)(2,1)S(1)} async-done(((bf16[8,32,640]{2,1,0:T(8,128)(2,1)}), bf16[8,32,640]{2,1,0:T(8,128)(2,1)S(1)}, u32[]{:S(2)}, u32[]{:S(2)}) %all-to-all-start) | async-done | bytes 327712 | tf_op jit(solution)/shard_map/all_to_all | solution.py:332
  27.8 4.6 %all-to-all-start.1 = ((bf16[8,64,640]{2,1,0:T(8,128)(2,1)}), bf16[8,64,640]{2,1,0:T(8,128)(2,1)S(1)}, u32[]{:S(2)}, u32[]{:S(2)}) async-start(bf16[8,64,640]{2,1,0:T(8,128)(2,1)} %shard_map.31), calls=%async_computation.1 | async-start | bytes 1310720 | tf_op jit(solution)/shard_map/all_to_all | solution.py:333
  32.3 10.8 %all-to-all-done.1.two = bf16[8,64,640]{2,1,0:T(8,128)(2,1)S(1)} async-done(((bf16[8,64,640]{2,1,0:T(8,128)(2,1)}), bf16[8,64,640]{2,1,0:T(8,128)(2,1)S(1)}, u32[]{:S(2)}, u32[]{:S(2)}) %all-to-all-start.1) | async-done | bytes 655392 | tf_op jit(solution)/shard_map/all_to_all | solution.py:333
  43.1 1.3 shard_map.32
  44.4 0.0 copy-start.1
  44.4 0.9 copy-done.1
  45.4 1.1 collective-permute-start.2
  46.4 1.8 %collective-permute-done.2 = f32[1408,128]{1,0:T(8,128)S(1)} collective-permute-done((f32[1408,128]{1,0:T(8,128)S(1)}, f32[1408,128]{1,0:T(8,128)S(1)}, u32[]{:S(2)}, u32[]{:S(2)}) %collective-permute-start.2) | collective-permute-done | bytes 720928 | tf_op jit(solution)/shard_map/ppermute | solution.py:153
  48.2 0.1 dynamic-slice_add_fusion
  48.4 0.2 collective-permute-start.3
  48.6 2.6 %collective-permute-start.5 = (f32[352,128]{1,0:T(8,128)S(1)}, f32[352,128]{1,0:T(8,128)S(1)}, u32[]{:S(2)}, u32[]{:S(2)}) collective-permute-start(f32[352,128]{1,0:T(8,128)S(1)} %get-tuple-element.19), channel_id=1, source_target_pairs={{0,192},{64,0},{128,64},{192,128},{1,193},{65,1},{129,65},{193,129... | collective-permute-start | bytes 540680 | tf_op jit(solution)/shard_map/ppermute | solution.py:173
  51.2 0.0 collective-permute-start.4
  51.2 4.5 %collective-permute-done.3 = f32[352,128]{1,0:T(8,128)S(1)} collective-permute-done((f32[352,128]{1,0:T(8,128)S(1)}, f32[352,128]{1,0:T(8,128)S(1)}, u32[]{:S(2)}, u32[]{:S(2)}) %collective-permute-start.3) | collective-permute-done | bytes 180256 | tf_op jit(solution)/shard_map/ppermute | solution.py:173
  55.7 2.3 %collective-permute-done.5 = f32[352,128]{1,0:T(8,128)S(1)} collective-permute-done((f32[352,128]{1,0:T(8,128)S(1)}, f32[352,128]{1,0:T(8,128)S(1)}, u32[]{:S(2)}, u32[]{:S(2)}) %collective-permute-start.5) | collective-permute-done | bytes 180256 | tf_op jit(solution)/shard_map/ppermute | solution.py:173
  58.1 2.0 %collective-permute-done.4 = f32[352,128]{1,0:T(8,128)S(1)} collective-permute-done((f32[352,128]{1,0:T(8,128)S(1)}, f32[352,128]{1,0:T(8,128)S(1)}, u32[]{:S(2)}, u32[]{:S(2)}) %collective-permute-start.4) | collective-permute-done | bytes 180256 | tf_op jit(solution)/shard_map/ppermute | solution.py:173
  60.1 19.9 %all_to_all.20 = f32[32,11,128]{2,1,0:T(8,128)S(1)} all-to-all(f32[32,11,128]{2,1,0:T(8,128)S(1)} %reshape.19), channel_id=1, replica_groups=mesh['x'=4,'c'=2,'y'=4,'z'=8] {'y','z'}, dimensions={0} | all-to-all | bytes 360448 | tf_op jit(solution)/shard_map/all_to_all | solution.py:192
  80.1 15.7 %all_to_all.21 = f32[32,11,128]{2,1,0:T(8,128)S(1)} all-to-all(f32[32,11,128]{2,1,0:T(8,128)S(1)} %broadcast_in_dim.13), channel_id=1, replica_groups=mesh['x'=4,'c'=2,'y'=4,'z'=8] {'y','z'}, dimensions={0} | all-to-all | bytes 360448 | tf_op jit(solution)/shard_map/all_to_all | solution.py:197
  95.7 0.1 collective-permute-start.6
  95.9 2.6 %collective-permute-start.8 = (f32[352,128]{1,0:T(8,128)S(1)}, f32[352,128]{1,0:T(8,128)S(1)}, u32[]{:S(2)}, u32[]{:S(2)}) collective-permute-start(f32[352,128]{1,0:T(8,128)S(1)} %reshape.20), channel_id=1, source_target_pairs={{0,192},{64,0},{128,64},{192,128},{1,193},{65,1},{129,65},{193,129... | collective-permute-start | bytes 540680 | tf_op jit(solution)/shard_map/ppermute | solution.py:184
  98.5 0.0 collective-permute-start.7
  98.6 2.8 %collective-permute-done.6 = f32[352,128]{1,0:T(8,128)S(1)} collective-permute-done((f32[352,128]{1,0:T(8,128)S(1)}, f32[352,128]{1,0:T(8,128)S(1)}, u32[]{:S(2)}, u32[]{:S(2)}) %collective-permute-start.6) | collective-permute-done | bytes 180256 | tf_op jit(solution)/shard_map/ppermute | solution.py:184
  101.4 3.8 %collective-permute-done.7 = f32[352,128]{1,0:T(8,128)S(1)} collective-permute-done((f32[352,128]{1,0:T(8,128)S(1)}, f32[352,128]{1,0:T(8,128)S(1)}, u32[]{:S(2)}, u32[]{:S(2)}) %collective-permute-start.7) | collective-permute-done | bytes 180256 | tf_op jit(solution)/shard_map/ppermute | solution.py:184
  105.2 0.0 collective-permute-done.8
  105.2 4.8 %collective-permute-start.9 = (f32[1408,128]{1,0:T(8,128)S(1)}, f32[1408,128]{1,0:T(8,128)S(1)}, u32[]{:S(2)}, u32[]{:S(2)}) collective-permute-start(f32[1408,128]{1,0:T(8,128)S(1)} %constant_dynamic-update-slice_fusion), channel_id=1, source_target_pairs={{0,32},{32,0},{1,33},{33,1},{2,34},{34,2},{3,35},{35,3},{4,36},{36... | collective-permute-start | bytes 2162696 | tf_op jit(solution)/shard_map/ppermute | solution.py:158
  110.0 1.8 %collective-permute-done.9 = f32[1408,128]{1,0:T(8,128)S(1)} collective-permute-done((f32[1408,128]{1,0:T(8,128)S(1)}, f32[1408,128]{1,0:T(8,128)S(1)}, u32[]{:S(2)}, u32[]{:S(2)}) %collective-permute-start.9) | collective-permute-done | bytes 720928 | tf_op jit(solution)/shard_map/ppermute | solution.py:158
  111.9 0.1 broadcast_select_fusion.1
  112.0 0.0 copy-start.2
  112.0 0.1 pad_maximum_fusion
  112.1 1.1 copy-done.2
  113.2 23.7 %shard_map.33 = (f32[768,768]{1,0:T(8,128)}, bf16[768,640]{1,0:T(8,128)(2,1)}) custom-call(f32[22,128,128]{2,1,0:T(8,128)S(1)} %bitcast.2, bf16[768,640]{1,0:T(8,128)(2,1)S(1)} %copy-done.2, f32[8,128]{1,0:T(8,128)S(1)} %broadcast_in_dim.14.ones), custom_call_target="tpu_custom_call" | custom-call | tf_op jit(solution)/shard_map/pallas_call | solution.py:319
  (14 shorter events, 0.4 us)
Async XLA Ops:
  0.6 9.4 %copy-start = (bf16[32,3,5,8,128]{4,3,2,1,0:T(8,128)(2,1)S(1)}, bf16[32,3,5,8,128]{4,3,2,1,0:T(8,128)(2,1)}, u32[]{:S(2)}) copy-start(bf16[32,3,5,8,128]{4,3,2,1,0:T(8,128)(2,1)} %vel.3) | copy-start | bytes 2949124
  3.0 17.7 %collective-permute-start.1 = (bf16[32,2,4,8,128]{4,3,2,1,0:T(8,128)(2,1)}, bf16[32,2,4,8,128]{4,3,2,1,0:T(8,128)(2,1)S(1)}, u32[]{:S(2)}, u32[]{:S(2)}) collective-permute-start(bf16[32,2,4,8,128]{4,3,2,1,0:T(8,128)(2,1)} %get-tuple-element.16), channel_id=1, source_target_pairs={{1,0},{2,1},{3,2},{4,3},{5,4},{6,5},{7,6},{8,7},{9,8},{10,9},{11,1... | collective-permute-start | bytes 1572872 | tf_op jit(solution)/shard_map/ppermute | solution.py:330
  4.3 16.4 %collective-permute-start = (bf16[32,2,4,8,128]{4,3,2,1,0:T(8,128)(2,1)}, bf16[32,2,4,8,128]{4,3,2,1,0:T(8,128)(2,1)}, u32[]{:S(2)}, u32[]{:S(2)}) collective-permute-start(bf16[32,2,4,8,128]{4,3,2,1,0:T(8,128)(2,1)} %get-tuple-element.17), channel_id=1, source_target_pairs={{0,1},{1,2},{2,3},{3,4},{4,5},{5,6},{6,7},{7,8},{8,9},{9,10},{10,1... | collective-permute-start | bytes 1572872 | tf_op jit(solution)/shard_map/ppermute | solution.py:329
  14.6 13.2 %all-to-all-start = ((bf16[8,32,640]{2,1,0:T(8,128)(2,1)}), bf16[8,32,640]{2,1,0:T(8,128)(2,1)S(1)}, u32[]{:S(2)}, u32[]{:S(2)}) async-start(bf16[8,32,640]{2,1,0:T(8,128)(2,1)} %get-tuple-element.8), calls=%async_computation | async-start | bytes 655360 | tf_op jit(solution)/shard_map/all_to_all | solution.py:332
  27.8 15.4 %all-to-all-start.1 = ((bf16[8,64,640]{2,1,0:T(8,128)(2,1)}), bf16[8,64,640]{2,1,0:T(8,128)(2,1)S(1)}, u32[]{:S(2)}, u32[]{:S(2)}) async-start(bf16[8,64,640]{2,1,0:T(8,128)(2,1)} %shard_map.31), calls=%async_computation.1 | async-start | bytes 1310720 | tf_op jit(solution)/shard_map/all_to_all | solution.py:333
  44.4 0.9 copy-start.1
  45.4 2.9 %collective-permute-start.2 = (f32[1408,128]{1,0:T(8,128)S(1)}, f32[1408,128]{1,0:T(8,128)S(1)}, u32[]{:S(2)}, u32[]{:S(2)}) collective-permute-start(f32[1408,128]{1,0:T(8,128)S(1)} %constant_dynamic-slice_fusion.3), channel_id=1, source_target_pairs={{0,32},{32,0},{1,33},{33,1},{2,34},{34,2},{3,35},{35,3},{4,36},{36... | collective-permute-start | bytes 2162696 | tf_op jit(solution)/shard_map/ppermute | solution.py:153
  48.4 7.3 %collective-permute-start.3 = (f32[352,128]{1,0:T(8,128)S(1)}, f32[352,128]{1,0:T(8,128)S(1)}, u32[]{:S(2)}, u32[]{:S(2)}) collective-permute-start(f32[352,128]{1,0:T(8,128)S(1)} %get-tuple-element.18), channel_id=1, source_target_pairs={{0,128},{64,192},{128,0},{192,64},{1,129},{65,193},{129,1},{193,65... | collective-permute-start | bytes 540680 | tf_op jit(solution)/shard_map/ppermute | solution.py:173
  48.6 9.5 %collective-permute-start.5 = (f32[352,128]{1,0:T(8,128)S(1)}, f32[352,128]{1,0:T(8,128)S(1)}, u32[]{:S(2)}, u32[]{:S(2)}) collective-permute-start(f32[352,128]{1,0:T(8,128)S(1)} %get-tuple-element.19), channel_id=1, source_target_pairs={{0,192},{64,0},{128,64},{192,128},{1,193},{65,1},{129,65},{193,129... | collective-permute-start | bytes 540680 | tf_op jit(solution)/shard_map/ppermute | solution.py:173
  51.2 8.9 %collective-permute-start.4 = (f32[352,128]{1,0:T(8,128)S(1)}, f32[352,128]{1,0:T(8,128)S(1)}, u32[]{:S(2)}, u32[]{:S(2)}) collective-permute-start(f32[352,128]{1,0:T(8,128)S(1)} %get-tuple-element.20), channel_id=1, source_target_pairs={{0,64},{64,128},{128,192},{192,0},{1,65},{65,129},{129,193},{193,1... | collective-permute-start | bytes 540680 | tf_op jit(solution)/shard_map/ppermute | solution.py:173
  95.7 5.6 %collective-permute-start.6 = (f32[352,128]{1,0:T(8,128)S(1)}, f32[352,128]{1,0:T(8,128)S(1)}, u32[]{:S(2)}, u32[]{:S(2)}) collective-permute-start(f32[352,128]{1,0:T(8,128)S(1)} %reshape.20), channel_id=1, source_target_pairs={{0,64},{64,128},{128,192},{192,0},{1,65},{65,129},{129,193},{193,1... | collective-permute-start | bytes 540680 | tf_op jit(solution)/shard_map/ppermute | solution.py:184
  95.9 9.3 %collective-permute-start.8 = (f32[352,128]{1,0:T(8,128)S(1)}, f32[352,128]{1,0:T(8,128)S(1)}, u32[]{:S(2)}, u32[]{:S(2)}) collective-permute-start(f32[352,128]{1,0:T(8,128)S(1)} %reshape.20), channel_id=1, source_target_pairs={{0,192},{64,0},{128,64},{192,128},{1,193},{65,1},{129,65},{193,129... | collective-permute-start | bytes 540680 | tf_op jit(solution)/shard_map/ppermute | solution.py:184
  98.5 6.7 %collective-permute-start.7 = (f32[352,128]{1,0:T(8,128)S(1)}, f32[352,128]{1,0:T(8,128)S(1)}, u32[]{:S(2)}, u32[]{:S(2)}) collective-permute-start(f32[352,128]{1,0:T(8,128)S(1)} %reshape.20), channel_id=1, source_target_pairs={{0,128},{64,192},{128,0},{192,64},{1,129},{65,193},{129,1},{193,65... | collective-permute-start | bytes 540680 | tf_op jit(solution)/shard_map/ppermute | solution.py:184
  105.2 6.6 %collective-permute-start.9 = (f32[1408,128]{1,0:T(8,128)S(1)}, f32[1408,128]{1,0:T(8,128)S(1)}, u32[]{:S(2)}, u32[]{:S(2)}) collective-permute-start(f32[1408,128]{1,0:T(8,128)S(1)} %constant_dynamic-update-slice_fusion), channel_id=1, source_target_pairs={{0,32},{32,0},{1,33},{33,1},{2,34},{34,2},{3,35},{35,3},{4,36},{36... | collective-permute-start | bytes 2162696 | tf_op jit(solution)/shard_map/ppermute | solution.py:158
  112.0 1.2 copy-start.2
where the time goes:
time: 137 us
  blocking collectives  35.6 us (26%)
  waiting for transfers between devices  34 us (25%)
  Pallas kernels  32.5 us (24%)
  starting transfers between devices  29 us (21%)
  local copies, waits for them, and re-layouts  4.63 us (3%)
    pallas_call x1, Pallas kernels, chol_solve(): pl.pallas_call(kernel, out_shape=(jax.ShapeDtypeStruct((768, 768), jnp.fl...  23.7 us
    all_to_all x1, blocking collectives, scatter_yz(): lax.all_to_all(v.reshape(32, -1, v.shape[1]), ('y', 'z'), 0, 0, tiled=True)  19.9 us
    all_to_all x1, blocking collectives, gather_yz(): lax.all_to_all(jnp.broadcast_to(v[None], (32,) + v.shape), ('y', 'z'), 0,...  15.7 us
    all_to_all x1, waiting for transfers between devices, body(): lax.all_to_all(outer(velocity, lo, hi, rest), ('x', 'c'), 0, 0, tiled=True)  10.8 us
    ppermute x3, waiting for transfers between devices, scatter_x(): got.append(lax.ppermute(send, 'x', ring(4, k)))  8.86 us
    ppermute x3, waiting for transfers between devices, gather_x(): parts[k] = lax.ppermute(v, 'x', ring(4, k))  6.57 us
    all_to_all x1, starting transfers between devices, body(): one = lax.all_to_all(share, ('x', 'c'), 0, 0, tiled=True)  6.09 us
    ppermute x1, starting transfers between devices, body(): lo = lax.ppermute(velocity[:, 1:, 1:5], ('y', 'z'), forward)  5.79 us
  transfers between devices with their start and end apart: 12, of which 9 were waited for; matrix products, arithmetic and copies ran while one was open for 0% of the time, Pallas kernels for 5%

commit v1 on v0

--- a/solution.py
+++ b/solution.py
@@ -12,6 +12,7 @@
 F32 = jnp.float32
 BF16 = jnp.bfloat16
 VM = pl.BlockSpec(memory_space=pltpu.VMEM)
+HBM = pl.BlockSpec(memory_space=pltpu.MemorySpace.HBM)
 
 
 def ramp(field, axis, coeffs):
@@ -68,7 +69,7 @@
         rest[1, s] = ramp(u, 1, ycs)
         return carry
 
-    lax.fori_loop(0, 32, one, 0)
+    lax.fori_loop(0, 32, one, 0, unroll=2)
     emit(buf, out, 32)
 
 
@@ -82,7 +83,7 @@
         place(buf, 32 + s, dxv - rest[1, s])
         return carry
 
-    lax.fori_loop(0, 32, one, 0)
+    lax.fori_loop(0, 32, one, 0, unroll=4)
     emit(buf, out, 64)
 
 
@@ -114,7 +115,7 @@
     return K * NB - K * (K - 1) // 2 + (J - K)
 
 
-def gram_kernel(one, two, m, out, buf):
+def gram_kernel(one, two, m_out, out, buf, m, sem):
     for j in range(5):
         cols = slice(j * 128, j * 128 + 128)
         for d in range(8):
@@ -122,6 +123,8 @@
             buf[j, pl.ds(96 * d + 1, 32, stride=3), :] = two[d, 0:32, cols].astype(F32)
             buf[j, pl.ds(96 * d + 2, 32, stride=3), :] = two[d, 32:64, cols].astype(F32)
         m[:, cols] = buf[j].astype(BF16)
+    copy = pltpu.make_async_copy(m, m_out, sem)
+    copy.start()
     for K in range(NB):
         rows = m[K * S : K * S + S, :]
         res = lax.dot_general(rows, m[K * S :, :], (((1,), (1,)), ((), ())), preferred_element_type=F32)
@@ -129,6 +132,7 @@
             b = block(K, J)
             out[b * S : b * S + S, :] = res[:, (J - K) * S : (J - K + 1) * S]
     out[21 * S :, :] = jnp.zeros((S, S), F32)
+    copy.wait()
 
 
 def gram_blocks(one, two):
@@ -136,8 +140,12 @@
         gram_kernel,
         out_shape=(jax.ShapeDtypeStruct((NB * S, 640), BF16), jax.ShapeDtypeStruct((22 * S, S), F32)),
         in_specs=[VM, VM],
-        out_specs=(VM, VM),
-        scratch_shapes=[pltpu.VMEM((5, NB * S, 128), F32)],
+        out_specs=(HBM, VM),
+        scratch_shapes=[
+            pltpu.VMEM((5, NB * S, 128), F32),
+            pltpu.VMEM((NB * S, 640), BF16),
+            pltpu.SemaphoreType.DMA(()),
+        ],
         compiler_params=pltpu.CompilerParams(vmem_limit_bytes=32 << 20),
     )(one, two)
 
@@ -155,8 +163,10 @@
 
 def gather_core(v):
     i = lax.axis_index("c")
+    h = v.shape[0]
     o = lax.ppermute(v, "c", SWAP)
-    return jnp.concatenate([jnp.where(i == 0, v, o), jnp.where(i == 0, o, v)], 0)
+    out = lax.dynamic_update_slice_in_dim(jnp.zeros((2 * h,) + v.shape[1:], v.dtype), v, i * h, 0)
+    return lax.dynamic_update_slice_in_dim(out, o, (1 - i) * h, 0)
 
 
 def ring(n, k):
@@ -249,6 +259,14 @@
         Rg=jnp.where(lanes>=rows+8*g,Dg*rsq,0.0); Tg=Wg*rsq
         D[8*g:8*g+8,:]=Rg
         T[8*g:8*g+8,:]=Tg
+        r0=8*(g+1+NV)
+        if r0<128:
+            p=[q.astype(jnp.float32) for q in parts(jnp.concatenate([Rg,Tg],axis=1))]
+            rr=jnp.concatenate([p[0],p[1],p[0],p[2],p[1],p[0]],axis=0).astype(BF)
+            ll=jnp.concatenate([p[i][:,:128] for i in (0,0,1,0,1,2)],axis=0)
+            upd=mm(jnp.transpose(ll)[r0:,:].astype(BF),rr)
+            D[r0:,:]=D[r0:,:]-upd[:,:128]
+            T[r0:,:]=T[r0:,:]-upd[:,128:]
         for h in range(g+1,min(g+1+NV,16)):
             Dh=D[8*h:8*h+8,:]; Wh=T[8*h:8*h+8,:]
             Bh=[lane(Dh,8*g+m) for m in range(8)]
@@ -257,16 +275,9 @@
                 for m in range(s+1,8): Bh[m]=Bh[m]-f*dm[m,s]
                 Dh=Dh-f*U[s]; Wh=Wh-f*V[s]
             D[8*h:8*h+8,:]=Dh; T[8*h:8*h+8,:]=Wh
-        r0=8*(g+1+NV)
-        if r0<128:
-            p=[q.astype(jnp.float32) for q in parts(jnp.concatenate([Rg,Tg],axis=1))]
-            rr=jnp.concatenate([p[0],p[1],p[0],p[2],p[1],p[0]],axis=0).astype(BF)
-            ll=jnp.concatenate([p[i][:,:128] for i in (0,0,1,0,1,2)],axis=0)
-            upd=mm(jnp.transpose(ll)[r0:,:].astype(BF),rr)
-            D[r0:,:]=D[r0:,:]-upd[:,:128]
-            T[r0:,:]=T[r0:,:]-upd[:,128:]
-def kernel(a_ref,m_ref,ones,f_ref,x_ref,A,T,M,TP,RT,RP,XP):
-    n=m_ref.shape[1]
+def chol_kernel(a_ref,m_hbm,ones,f_ref,x_ref,A,T,M,TP,RT,RP,XP,m_ref,sem):
+    bring=pltpu.make_async_copy(m_hbm,m_ref,sem)
+    bring.start()
     def zero():
         for K in range(NB):
             if K: f_ref[K*S:K*S+S,0:K*S]=jnp.zeros((S,K*S),jnp.float32)
@@ -279,7 +290,7 @@
         if K==0:
             Dk[...]=a_ref[0]
         diag(Dk,T,ones,fill)
-        assert not fill
+        if K==0: bring.wait()
         f_ref[K*S:K*S+S,K*S:K*S+S]=Dk[...]
         put(TP,parts(T[...]))
         src=a_ref if K==0 else A
@@ -316,9 +327,9 @@
 def chol_solve(blocks,m):
     n=m.shape[1]
     vm=pl.BlockSpec(memory_space=pltpu.VMEM)
-    return pl.pallas_call(kernel,out_shape=(jax.ShapeDtypeStruct((768,768),jnp.float32),jax.ShapeDtypeStruct((768,n),jnp.bfloat16)),
-        in_specs=[vm,vm,vm],out_specs=(vm,vm),
-        scratch_shapes=[pltpu.VMEM((21,S,S),jnp.float32),pltpu.VMEM((S,S),jnp.float32),pltpu.VMEM((768,n),jnp.float32),pltpu.VMEM((3,S,S),BF),pltpu.VMEM((NB,3,S,S),BF),pltpu.VMEM((NB,3,S,S),BF),pltpu.VMEM((3,S,n),BF)],
+    return pl.pallas_call(chol_kernel,out_shape=(jax.ShapeDtypeStruct((768,768),jnp.float32),jax.ShapeDtypeStruct((768,n),jnp.bfloat16)),
+        in_specs=[vm,HBM,vm],out_specs=(vm,vm),
+        scratch_shapes=[pltpu.VMEM((21,S,S),jnp.float32),pltpu.VMEM((S,S),jnp.float32),pltpu.VMEM((768,n),jnp.float32),pltpu.VMEM((3,S,S),BF),pltpu.VMEM((NB,3,S,S),BF),pltpu.VMEM((NB,3,S,S),BF),pltpu.VMEM((3,S,n),BF),pltpu.VMEM((768,n),BF),pltpu.SemaphoreType.DMA(())],
         compiler_params=pltpu.CompilerParams(vmem_limit_bytes=40<<20))(blocks,m,jnp.ones((8,128),jnp.float32))
 
 

time: 137 us -> 136 us (level)
    ppermute x1, waiting for transfers between devices: 0.01 us -> 4.17 us  [body(): hi = lax.ppermute(velocity[:, 1:, 0:4], ('y', 'z'), backward)]
    all_to_all x1, waiting for transfers between devices: 4.15 us -> 0.01 us  [body(): one = lax.all_to_all(share, ('x', 'c'), 0, 0, tiled=True)]
    ppermute x3, waiting for transfers between devices: 6.57 us -> 4.89 us  [gather_x(): parts[k] = lax.ppermute(v, 'x', ring(4, k))]
    ppermute x1, starting transfers between devices: 5.79 us -> 4.38 us  [body(): lo = lax.ppermute(velocity[:, 1:, 1:5], ('y', 'z'), forward)]
    all_to_all x1, starting transfers between devices: 4.57 us -> 5.95 us  [body(): lax.all_to_all(outer(velocity, lo, hi, rest), ('x', 'c'), 0, 0, tiled=True)]
where the time goes in v1:
time: 136 us
  blocking collectives  36.2 us (27%)
  waiting for transfers between devices  32.9 us (24%)
  Pallas kernels  32.5 us (24%)
  starting transfers between devices  29.1 us (21%)
  local copies, waits for them, and re-layouts  3.75 us (3%)
    pallas_call x1, Pallas kernels, chol_solve(): pl.pallas_call(chol_kernel, out_shape=(jax.ShapeDtypeStruct((768, 768), j...  24.7 us
    all_to_all x1, blocking collectives, scatter_yz(): lax.all_to_all(v.reshape(32, -1, v.shape[1]), ('y', 'z'), 0, 0, tiled=True)  20.4 us
    all_to_all x1, blocking collectives, gather_yz(): lax.all_to_all(jnp.broadcast_to(v[None], (32,) + v.shape), ('y', 'z'), 0,...  15.8 us
    all_to_all x1, waiting for transfers between devices, body(): lax.all_to_all(outer(velocity, lo, hi, rest), ('x', 'c'), 0, 0, tiled=True)  10.8 us
    ppermute x3, waiting for transfers between devices, scatter_x(): got.append(lax.ppermute(send, 'x', ring(4, k)))  8.68 us
    all_to_all x1, starting transfers between devices, body(): lax.all_to_all(outer(velocity, lo, hi, rest), ('x', 'c'), 0, 0, tiled=True)  5.95 us
    all_to_all x1, starting transfers between devices, body(): one = lax.all_to_all(share, ('x', 'c'), 0, 0, tiled=True)  5.25 us
    ppermute x3, waiting for transfers between devices, gather_x(): parts[k] = lax.ppermute(v, 'x', ring(4, k))  4.89 us
  transfers between devices with their start and end apart: 12, of which 9 were waited for; matrix products, arithmetic and copies ran while one was open for 0% of the time, Pallas kernels for 5%

profile of v1, /device:TPU:1, one launch (start us, length us, event | category | flops | bytes accessed | tf_op | source)
XLA Modules:
  0.0 135.6 jit_solution(3871199895956721675)
XLA Ops:
  0.6 0.0 copy-start
  0.6 2.3 %fusion = (bf16[32,2,4,8,128]{4,3,2,1,0:T(8,128)(2,1)}, bf16[32,2,4,8,128]{4,3,2,1,0:T(8,128)(2,1)}) fusion(bf16[32,3,5,8,128]{4,3,2,1,0:T(8,128)(2,1)} %vel.3), kind=kLoop, calls=%fused_computation.13 | loop fusion | bytes 2097152 | tf_op jit(solution)/shard_map/slice | solution.py:341
  3.0 4.4 %collective-permute-start = (bf16[32,2,4,8,128]{4,3,2,1,0:T(8,128)(2,1)}, bf16[32,2,4,8,128]{4,3,2,1,0:T(8,128)(2,1)S(1)}, u32[]{:S(2)}, u32[]{:S(2)}) collective-permute-start(bf16[32,2,4,8,128]{4,3,2,1,0:T(8,128)(2,1)} %get-tuple-element.15), channel_id=1, source_target_pairs={{0,1},{1,2},{2,3},{3,4},{4,5},{5,6},{6,7},{7,8},{8,9},{9,10},{10,1... | collective-permute-start | bytes 1572872 | tf_op jit(solution)/shard_map/ppermute | solution.py:340
  7.4 1.3 collective-permute-start.1
  8.7 0.0 copy-done
  8.7 3.4 %shard_map.30 = (bf16[8,32,640]{2,1,0:T(8,128)(2,1)}, f32[2,32,5,8,128]{4,3,2,1,0:T(8,128)S(1)}) custom-call(bf16[32,3,5,8,128]{4,3,2,1,0:T(8,128)(2,1)S(1)} %copy-done), custom_call_target="tpu_custom_call" | custom-call | flops 10000000 | bytes 12000000 | tf_op jit(solution)/shard_map/pallas_call | solution.py:91
  12.0 5.3 %all-to-all-start = ((bf16[8,32,640]{2,1,0:T(8,128)(2,1)}), bf16[8,32,640]{2,1,0:T(8,128)(2,1)S(1)}, u32[]{:S(2)}, u32[]{:S(2)}) async-start(bf16[8,32,640]{2,1,0:T(8,128)(2,1)} %get-tuple-element.8), calls=%async_computation | async-start | bytes 655360 | tf_op jit(solution)/shard_map/all_to_all | solution.py:343
  17.3 0.9 collective-permute-done.lo
  18.2 4.2 %collective-permute-done.1.hi = bf16[32,2,4,8,128]{4,3,2,1,0:T(8,128)(2,1)} collective-permute-done((bf16[32,2,4,8,128]{4,3,2,1,0:T(8,128)(2,1)}, bf16[32,2,4,8,128]{4,3,2,1,0:T(8,128)(2,1)}, u32[]{:S(2)}, u32[]{:S(2)}) %collective-permute-start.1) | collective-permute-done | bytes 524320 | tf_op jit(solution)/shard_map/ppermute | solution.py:341
  22.4 2.8 %shard_map.31 = bf16[8,64,640]{2,1,0:T(8,128)(2,1)} custom-call(bf16[32,3,5,8,128]{4,3,2,1,0:T(8,128)(2,1)S(1)} %copy-done, bf16[32,2,4,8,128]{4,3,2,1,0:T(8,128)(2,1)S(1)} %collective-permute-done.lo, bf16[32,2,4,8,128]{4,3,2,1,0:T(8,128)(2,1)} %collective-permute-done.1.hi, f32[2,32,5,8,128]{4,3,2,1,0:T(8,128)S(1)} %get-tuple-element.9.rest), custom_call_target="tpu_custom_call" | custom-call | flops 10000000 | bytes 6000000 | tf_op jit(solution)/shard_map/pallas_call | solution.py:103
  25.2 0.0 all-to-all-done.one
  25.2 6.0 %all-to-all-start.1 = ((bf16[8,64,640]{2,1,0:T(8,128)(2,1)}), bf16[8,64,640]{2,1,0:T(8,128)(2,1)S(1)}, u32[]{:S(2)}, u32[]{:S(2)}) async-start(bf16[8,64,640]{2,1,0:T(8,128)(2,1)} %shard_map.31), calls=%async_computation.1 | async-start | bytes 1310720 | tf_op jit(solution)/shard_map/all_to_all | solution.py:344
  31.2 10.8 %all-to-all-done.1.two = bf16[8,64,640]{2,1,0:T(8,128)(2,1)S(1)} async-done(((bf16[8,64,640]{2,1,0:T(8,128)(2,1)}), bf16[8,64,640]{2,1,0:T(8,128)(2,1)S(1)}, u32[]{:S(2)}, u32[]{:S(2)}) %all-to-all-start.1) | async-done | bytes 655392 | tf_op jit(solution)/shard_map/all_to_all | solution.py:344
  41.9 1.7 %shard_map.32 = (bf16[768,640]{1,0:T(8,128)(2,1)S(1)}, f32[2816,128]{1,0:T(8,128)S(1)}) custom-call(bf16[8,32,640]{2,1,0:T(8,128)(2,1)S(1)} %all-to-all-done.one, bf16[8,64,640]{2,1,0:T(8,128)(2,1)S(1)} %all-to-all-done.1.two), custom_call_target="tpu_custom_call" | custom-call | tf_op jit(solution)/shard_map/pallas_call | solution.py:139
  43.6 0.0 copy-start.1
  43.6 0.9 copy-done.1
  44.6 1.1 collective-permute-start.2
  45.7 1.8 %collective-permute-done.2 = f32[1408,128]{1,0:T(8,128)S(1)} collective-permute-done((f32[1408,128]{1,0:T(8,128)S(1)}, f32[1408,128]{1,0:T(8,128)S(1)}, u32[]{:S(2)}, u32[]{:S(2)}) %collective-permute-start.2) | collective-permute-done | bytes 720928 | tf_op jit(solution)/shard_map/ppermute | solution.py:161
  47.5 0.1 dynamic-slice_add_fusion
  47.6 0.2 collective-permute-start.3
  47.8 1.4 collective-permute-start.4
  49.2 1.3 collective-permute-start.5
  50.5 4.5 %collective-permute-done.3 = f32[352,128]{1,0:T(8,128)S(1)} collective-permute-done((f32[352,128]{1,0:T(8,128)S(1)}, f32[352,128]{1,0:T(8,128)S(1)}, u32[]{:S(2)}, u32[]{:S(2)}) %collective-permute-start.3) | collective-permute-done | bytes 180256 | tf_op jit(solution)/shard_map/ppermute | solution.py:183
  55.0 4.2 %collective-permute-done.4 = f32[352,128]{1,0:T(8,128)S(1)} collective-permute-done((f32[352,128]{1,0:T(8,128)S(1)}, f32[352,128]{1,0:T(8,128)S(1)}, u32[]{:S(2)}, u32[]{:S(2)}) %collective-permute-start.4) | collective-permute-done | bytes 180256 | tf_op jit(solution)/shard_map/ppermute | solution.py:183
  59.2 0.0 collective-permute-done.5
  59.3 20.4 %all_to_all.20 = f32[32,11,128]{2,1,0:T(8,128)S(1)} all-to-all(f32[32,11,128]{2,1,0:T(8,128)S(1)} %reshape.19), channel_id=1, replica_groups=mesh['x'=4,'c'=2,'y'=4,'z'=8] {'y','z'}, dimensions={0} | all-to-all | bytes 360448 | tf_op jit(solution)/shard_map/all_to_all | solution.py:202
  79.7 15.8 %all_to_all.21 = f32[32,11,128]{2,1,0:T(8,128)S(1)} all-to-all(f32[32,11,128]{2,1,0:T(8,128)S(1)} %broadcast_in_dim.17), channel_id=1, replica_groups=mesh['x'=4,'c'=2,'y'=4,'z'=8] {'y','z'}, dimensions={0} | all-to-all | bytes 360448 | tf_op jit(solution)/shard_map/all_to_all | solution.py:207
  95.5 0.8 collective-permute-start.6
  96.4 1.8 %collective-permute-start.7 = (f32[352,128]{1,0:T(8,128)S(1)}, f32[352,128]{1,0:T(8,128)S(1)}, u32[]{:S(2)}, u32[]{:S(2)}) collective-permute-start(f32[352,128]{1,0:T(8,128)S(1)} %reshape.20), channel_id=1, source_target_pairs={{0,128},{64,192},{128,0},{192,64},{1,129},{65,193},{129,1},{193,65... | collective-permute-start | bytes 540680 | tf_op jit(solution)/shard_map/ppermute | solution.py:194
  98.1 0.8 collective-permute-start.8
  99.0 4.1 %collective-permute-done.6 = f32[352,128]{1,0:T(8,128)S(1)} collective-permute-done((f32[352,128]{1,0:T(8,128)S(1)}, f32[352,128]{1,0:T(8,128)S(1)}, u32[]{:S(2)}, u32[]{:S(2)}) %collective-permute-start.6) | collective-permute-done | bytes 180256 | tf_op jit(solution)/shard_map/ppermute | solution.py:194
  103.1 0.0 collective-permute-done.7
  103.1 0.8 collective-permute-done.8
  104.0 4.9 %collective-permute-start.9 = (f32[1408,128]{1,0:T(8,128)S(1)}, f32[1408,128]{1,0:T(8,128)S(1)}, u32[]{:S(2)}, u32[]{:S(2)}) collective-permute-start(f32[1408,128]{1,0:T(8,128)S(1)} %constant_dynamic-update-slice_fusion.2), channel_id=1, source_target_pairs={{0,32},{32,0},{1,33},{33,1},{2,34},{34,2},{3,35},{35,3},{4,36},{36... | collective-permute-start | bytes 2162696 | tf_op jit(solution)/shard_map/ppermute | solution.py:167
  108.9 0.1 broadcast_in_dim.15
  109.0 0.0 copy-start.2
  109.0 0.1 constant_dynamic-update-slice_fusion.1
  109.0 1.6 %collective-permute-done.9 = f32[1408,128]{1,0:T(8,128)S(1)} collective-permute-done((f32[1408,128]{1,0:T(8,128)S(1)}, f32[1408,128]{1,0:T(8,128)S(1)}, u32[]{:S(2)}, u32[]{:S(2)}) %collective-permute-start.9) | collective-permute-done | bytes 720928 | tf_op jit(solution)/shard_map/ppermute | solution.py:167
  110.7 0.1 constant_dynamic-update-slice_fusion
  110.8 0.0 copy-done.2
  110.8 24.7 %shard_map.33 = (f32[768,768]{1,0:T(8,128)}, bf16[768,640]{1,0:T(8,128)(2,1)}) custom-call(f32[22,128,128]{2,1,0:T(8,128)S(1)} %bitcast.2, bf16[768,640]{1,0:T(8,128)(2,1)S(1)} %copy-done.2, f32[8,128]{1,0:T(8,128)S(1)} %broadcast_in_dim.18.ones), custom_call_target="tpu_custom_call" | custom-call | tf_op jit(solution)/shard_map/pallas_call | solution.py:330
  (14 shorter events, 0.4 us)
Async XLA Ops:
  0.6 8.0 %copy-start = (bf16[32,3,5,8,128]{4,3,2,1,0:T(8,128)(2,1)S(1)}, bf16[32,3,5,8,128]{4,3,2,1,0:T(8,128)(2,1)}, u32[]{:S(2)}) copy-start(bf16[32,3,5,8,128]{4,3,2,1,0:T(8,128)(2,1)} %vel.3) | copy-start | bytes 2949124
  3.0 15.3 %collective-permute-start = (bf16[32,2,4,8,128]{4,3,2,1,0:T(8,128)(2,1)}, bf16[32,2,4,8,128]{4,3,2,1,0:T(8,128)(2,1)S(1)}, u32[]{:S(2)}, u32[]{:S(2)}) collective-permute-start(bf16[32,2,4,8,128]{4,3,2,1,0:T(8,128)(2,1)} %get-tuple-element.15), channel_id=1, source_target_pairs={{0,1},{1,2},{2,3},{3,4},{4,5},{5,6},{6,7},{7,8},{8,9},{9,10},{10,1... | collective-permute-start | bytes 1572872 | tf_op jit(solution)/shard_map/ppermute | solution.py:340
  7.4 15.0 %collective-permute-start.1 = (bf16[32,2,4,8,128]{4,3,2,1,0:T(8,128)(2,1)}, bf16[32,2,4,8,128]{4,3,2,1,0:T(8,128)(2,1)}, u32[]{:S(2)}, u32[]{:S(2)}) collective-permute-start(bf16[32,2,4,8,128]{4,3,2,1,0:T(8,128)(2,1)} %get-tuple-element.14), channel_id=1, source_target_pairs={{1,0},{2,1},{3,2},{4,3},{5,4},{6,5},{7,6},{8,7},{9,8},{10,9},{11,1... | collective-permute-start | bytes 1572872 | tf_op jit(solution)/shard_map/ppermute | solution.py:341
  12.0 13.2 %all-to-all-start = ((bf16[8,32,640]{2,1,0:T(8,128)(2,1)}), bf16[8,32,640]{2,1,0:T(8,128)(2,1)S(1)}, u32[]{:S(2)}, u32[]{:S(2)}) async-start(bf16[8,32,640]{2,1,0:T(8,128)(2,1)} %get-tuple-element.8), calls=%async_computation | async-start | bytes 655360 | tf_op jit(solution)/shard_map/all_to_all | solution.py:343
  25.2 16.7 %all-to-all-start.1 = ((bf16[8,64,640]{2,1,0:T(8,128)(2,1)}), bf16[8,64,640]{2,1,0:T(8,128)(2,1)S(1)}, u32[]{:S(2)}, u32[]{:S(2)}) async-start(bf16[8,64,640]{2,1,0:T(8,128)(2,1)} %shard_map.31), calls=%async_computation.1 | async-start | bytes 1310720 | tf_op jit(solution)/shard_map/all_to_all | solution.py:344
  43.6 0.9 copy-start.1
  44.6 2.9 %collective-permute-start.2 = (f32[1408,128]{1,0:T(8,128)S(1)}, f32[1408,128]{1,0:T(8,128)S(1)}, u32[]{:S(2)}, u32[]{:S(2)}) collective-permute-start(f32[1408,128]{1,0:T(8,128)S(1)} %constant_dynamic-slice_fusion.3), channel_id=1, source_target_pairs={{0,32},{32,0},{1,33},{33,1},{2,34},{34,2},{3,35},{35,3},{4,36},{36... | collective-permute-start | bytes 2162696 | tf_op jit(solution)/shard_map/ppermute | solution.py:161
  47.6 7.4 %collective-permute-start.3 = (f32[352,128]{1,0:T(8,128)S(1)}, f32[352,128]{1,0:T(8,128)S(1)}, u32[]{:S(2)}, u32[]{:S(2)}) collective-permute-start(f32[352,128]{1,0:T(8,128)S(1)} %get-tuple-element.16), channel_id=1, source_target_pairs={{0,128},{64,192},{128,0},{192,64},{1,129},{65,193},{129,1},{193,65... | collective-permute-start | bytes 540680 | tf_op jit(solution)/shard_map/ppermute | solution.py:183
  47.8 11.4 %collective-permute-start.4 = (f32[352,128]{1,0:T(8,128)S(1)}, f32[352,128]{1,0:T(8,128)S(1)}, u32[]{:S(2)}, u32[]{:S(2)}) collective-permute-start(f32[352,128]{1,0:T(8,128)S(1)} %get-tuple-element.18), channel_id=1, source_target_pairs={{0,64},{64,128},{128,192},{192,0},{1,65},{65,129},{129,193},{193,1... | collective-permute-start | bytes 540680 | tf_op jit(solution)/shard_map/ppermute | solution.py:183
  49.2 10.0 %collective-permute-start.5 = (f32[352,128]{1,0:T(8,128)S(1)}, f32[352,128]{1,0:T(8,128)S(1)}, u32[]{:S(2)}, u32[]{:S(2)}) collective-permute-start(f32[352,128]{1,0:T(8,128)S(1)} %get-tuple-element.17), channel_id=1, source_target_pairs={{0,192},{64,0},{128,64},{192,128},{1,193},{65,1},{129,65},{193,129... | collective-permute-start | bytes 540680 | tf_op jit(solution)/shard_map/ppermute | solution.py:183
  95.5 7.6 %collective-permute-start.6 = (f32[352,128]{1,0:T(8,128)S(1)}, f32[352,128]{1,0:T(8,128)S(1)}, u32[]{:S(2)}, u32[]{:S(2)}) collective-permute-start(f32[352,128]{1,0:T(8,128)S(1)} %reshape.20), channel_id=1, source_target_pairs={{0,64},{64,128},{128,192},{192,0},{1,65},{65,129},{129,193},{193,1... | collective-permute-start | bytes 540680 | tf_op jit(solution)/shard_map/ppermute | solution.py:194
  96.4 6.7 %collective-permute-start.7 = (f32[352,128]{1,0:T(8,128)S(1)}, f32[352,128]{1,0:T(8,128)S(1)}, u32[]{:S(2)}, u32[]{:S(2)}) collective-permute-start(f32[352,128]{1,0:T(8,128)S(1)} %reshape.20), channel_id=1, source_target_pairs={{0,128},{64,192},{128,0},{192,64},{1,129},{65,193},{129,1},{193,65... | collective-permute-start | bytes 540680 | tf_op jit(solution)/shard_map/ppermute | solution.py:194
  98.1 5.8 %collective-permute-start.8 = (f32[352,128]{1,0:T(8,128)S(1)}, f32[352,128]{1,0:T(8,128)S(1)}, u32[]{:S(2)}, u32[]{:S(2)}) collective-permute-start(f32[352,128]{1,0:T(8,128)S(1)} %reshape.20), channel_id=1, source_target_pairs={{0,192},{64,0},{128,64},{192,128},{1,193},{65,1},{129,65},{193,129... | collective-permute-start | bytes 540680 | tf_op jit(solution)/shard_map/ppermute | solution.py:194
  104.0 6.7 %collective-permute-start.9 = (f32[1408,128]{1,0:T(8,128)S(1)}, f32[1408,128]{1,0:T(8,128)S(1)}, u32[]{:S(2)}, u32[]{:S(2)}) collective-permute-start(f32[1408,128]{1,0:T(8,128)S(1)} %constant_dynamic-update-slice_fusion.2), channel_id=1, source_target_pairs={{0,32},{32,0},{1,33},{33,1},{2,34},{34,2},{3,35},{35,3},{4,36},{36... | collective-permute-start | bytes 2162696 | tf_op jit(solution)/shard_map/ppermute | solution.py:167
  109.0 1.8 %copy-start.2 = (bf16[768,640]{1,0:T(8,128)(2,1)S(1)}, bf16[768,640]{1,0:T(8,128)(2,1)}, u32[]{:S(2)}) copy-start(bf16[768,640]{1,0:T(8,128)(2,1)} %copy-done.1) | copy-start | bytes 2949124

commit v2 on v1

--- a/solution.py
+++ b/solution.py
@@ -12,7 +12,6 @@
 F32 = jnp.float32
 BF16 = jnp.bfloat16
 VM = pl.BlockSpec(memory_space=pltpu.VMEM)
-HBM = pl.BlockSpec(memory_space=pltpu.MemorySpace.HBM)
 
 
 def ramp(field, axis, coeffs):
@@ -111,40 +110,53 @@
     )(vel, lo, hi, rest)
 
 
-def block(K, J):
-    return K * NB - K * (K - 1) // 2 + (J - K)
-
-
-def gram_kernel(one, two, m_out, out, buf, m, sem):
-    for j in range(5):
+SHARE = 296
+
+
+def above(K, J):
+    return K * NB - K * (K + 1) // 2 + (J - K - 1)
+
+
+def weave(one, two, m, buf, js):
+    for j in js:
         cols = slice(j * 128, j * 128 + 128)
         for d in range(8):
             buf[j, pl.ds(96 * d, 32, stride=3), :] = one[d, :, cols].astype(F32)
             buf[j, pl.ds(96 * d + 1, 32, stride=3), :] = two[d, 0:32, cols].astype(F32)
             buf[j, pl.ds(96 * d + 2, 32, stride=3), :] = two[d, 32:64, cols].astype(F32)
         m[:, cols] = buf[j].astype(BF16)
-    copy = pltpu.make_async_copy(m, m_out, sem)
-    copy.start()
+
+
+def gram_kernel(one, two, out, buf, m):
+    weave(one, two, m, buf, range(5))
+    r = lax.broadcasted_iota(jnp.int32, (S, S), 0)
+    c = lax.broadcasted_iota(jnp.int32, (S, S), 1)
+    out[18 * S :, :] = jnp.zeros((8 * SHARE - 18 * S, S), F32)
+    even = None
     for K in range(NB):
         rows = m[K * S : K * S + S, :]
         res = lax.dot_general(rows, m[K * S :, :], (((1,), (1,)), ((), ())), preferred_element_type=F32)
-        for J in range(K, NB):
-            b = block(K, J)
+        first = res[:, 0:S]
+        if K % 2 == 0:
+            even = first
+        else:
+            p = K // 2
+            out[(15 + p) * S : (16 + p) * S, :] = jnp.where(r <= c, even, first)
+            out[18 * S + p : 18 * S + p + 1, :] = jnp.sum(jnp.where(r == c, first, 0.0), axis=0, keepdims=True)
+        for J in range(K + 1, NB):
+            b = above(K, J)
             out[b * S : b * S + S, :] = res[:, (J - K) * S : (J - K + 1) * S]
-    out[21 * S :, :] = jnp.zeros((S, S), F32)
-    copy.wait()
 
 
 def gram_blocks(one, two):
     return pl.pallas_call(
         gram_kernel,
-        out_shape=(jax.ShapeDtypeStruct((NB * S, 640), BF16), jax.ShapeDtypeStruct((22 * S, S), F32)),
+        out_shape=jax.ShapeDtypeStruct((8 * SHARE, S), F32),
         in_specs=[VM, VM],
-        out_specs=(HBM, VM),
+        out_specs=VM,
         scratch_shapes=[
             pltpu.VMEM((5, NB * S, 128), F32),
             pltpu.VMEM((NB * S, 640), BF16),
-            pltpu.SemaphoreType.DMA(()),
         ],
         compiler_params=pltpu.CompilerParams(vmem_limit_bytes=32 << 20),
     )(one, two)
@@ -199,13 +211,14 @@
 
 
 def scatter_yz(v):
+    v = jnp.pad(v, ((0, 320 - SHARE), (0, 0)))
     got = lax.all_to_all(v.reshape(32, -1, v.shape[1]), ("y", "z"), 0, 0, tiled=True)
     return got.sum(0)
 
 
 def gather_yz(v):
     got = lax.all_to_all(jnp.broadcast_to(v[None], (32,) + v.shape), ("y", "z"), 0, 0, tiled=True)
-    return got.reshape(-1, v.shape[1])
+    return got.reshape(-1, v.shape[1])[:SHARE]
 
 
 def total_of(v):
@@ -275,32 +288,41 @@
                 for m in range(s+1,8): Bh[m]=Bh[m]-f*dm[m,s]
                 Dh=Dh-f*U[s]; Wh=Wh-f*V[s]
             D[8*h:8*h+8,:]=Dh; T[8*h:8*h+8,:]=Wh
-def chol_kernel(a_ref,m_hbm,ones,f_ref,x_ref,A,T,M,TP,RT,RP,XP,m_ref,sem):
-    bring=pltpu.make_async_copy(m_hbm,m_ref,sem)
-    bring.start()
+def chol_kernel(a_ref,one,two,ones,f_out,x_out,A,T,M,TP,RT,RP,XP,m_ref,wb,f_ref,x_ref,sems):
+    top=slice(0,4*S); low=slice(4*S,NB*S)
+    outs=[pltpu.make_async_copy(v.at[r],o.at[r],sems.at[i]) for i,(v,o,r) in enumerate(((f_ref,f_out,top),(x_ref,x_out,top),(f_ref,f_out,low),(x_ref,x_out,low)))]
     def zero():
         for K in range(NB):
             if K: f_ref[K*S:K*S+S,0:K*S]=jnp.zeros((S,K*S),jnp.float32)
-    fill=[]
+    r_=lax.broadcasted_iota(jnp.int32,(S,S),0); c_=lax.broadcasted_iota(jnp.int32,(S,S),1)
+    def tile(b): return a_ref[b*S:b*S+S,:]
+    def unpack(p,ks):
+        t=tile(15+p); u=jnp.transpose(t)
+        if 0 in ks: A[bi(2*p,2*p)]=jnp.where(r_<=c_,t,u)
+        if 1 in ks:
+            v=jnp.where(r_>c_,t,u)
+            A[bi(2*p+1,2*p+1)]=jnp.where(r_==c_,a_ref[18*S+p:18*S+p+1,:],v)
+    def base(K,I,J):
+        return tile(above(I,J)) if K==0 and I!=J else A[bi(I,J)]
+    unpack(0,(0,1))
+    fill=[lambda p=p: unpack(p,(0,1)) for p in (1,2)]+[lambda j=j: weave(one,two,m_ref,wb,[j]) for j in range(5)]
     def put(ref,p):
         for i in range(3): ref[i]=p[i]
     def get(ref): return ref[0],ref[1],ref[2]
     for K in range(NB):
         Dk=A.at[bi(K,K)]
-        if K==0:
-            Dk[...]=a_ref[0]
         diag(Dk,T,ones,fill)
-        if K==0: bring.wait()
+        if K==4:
+            outs[0].start(); outs[1].start()
         f_ref[K*S:K*S+S,K*S:K*S+S]=Dk[...]
         put(TP,parts(T[...]))
-        src=a_ref if K==0 else A
-        def panel(J,K=K,src=src):
-            r=mm(left(get(TP)),right(parts(src[bi(K,J)])))
+        def panel(J,K=K):
+            r=mm(left(get(TP)),right(parts(base(K,K,J))))
             f_ref[K*S:K*S+S,J*S:J*S+S]=r
             put(RT.at[J],parts(jnp.transpose(r))); put(RP.at[J],parts(r))
-        def update(I,J,K=K,src=src):
+        def update(I,J,K=K):
             b=bi(I,J)
-            A[b]=src[b]-mm(left(get(RT.at[I])),right(get(RP.at[J])))
+            A[b]=base(K,I,J)-mm(left(get(RT.at[I])),right(get(RP.at[J])))
         def solve(K=K):
             tp=get(TP)
             if K==0:
@@ -314,7 +336,10 @@
             m0=m_ref[I*S:I*S+S,:].astype(jnp.float32) if K==0 else M[I*S:I*S+S,:]
             M[I*S:I*S+S,:]=m0-mm(left(get(RT.at[I])),right(get(XP)))
         if K==NB-1:
-            solve(); break
+            solve()
+            outs[2].start(); outs[3].start()
+            for o in outs: o.wait()
+            break
         panel(K+1)
         update(K+1,K+1)
         if K==0: fill.append(zero)
@@ -324,13 +349,13 @@
             for J in range(I,NB):
                 if J>K+1: fill.append(lambda I=I,J=J,f=update: f(I,J))
             fill.append(lambda I=I,f=updm: f(I))
-def chol_solve(blocks,m):
-    n=m.shape[1]
+def chol_solve(blocks,one,two):
+    n=one.shape[2]
     vm=pl.BlockSpec(memory_space=pltpu.VMEM)
     return pl.pallas_call(chol_kernel,out_shape=(jax.ShapeDtypeStruct((768,768),jnp.float32),jax.ShapeDtypeStruct((768,n),jnp.bfloat16)),
-        in_specs=[vm,HBM,vm],out_specs=(vm,vm),
-        scratch_shapes=[pltpu.VMEM((21,S,S),jnp.float32),pltpu.VMEM((S,S),jnp.float32),pltpu.VMEM((768,n),jnp.float32),pltpu.VMEM((3,S,S),BF),pltpu.VMEM((NB,3,S,S),BF),pltpu.VMEM((NB,3,S,S),BF),pltpu.VMEM((3,S,n),BF),pltpu.VMEM((768,n),BF),pltpu.SemaphoreType.DMA(())],
-        compiler_params=pltpu.CompilerParams(vmem_limit_bytes=40<<20))(blocks,m,jnp.ones((8,128),jnp.float32))
+        in_specs=[vm,vm,vm,vm],out_specs=(pl.BlockSpec(memory_space=pl.ANY),pl.BlockSpec(memory_space=pl.ANY)),
+        scratch_shapes=[pltpu.VMEM((21,S,S),jnp.float32),pltpu.VMEM((S,S),jnp.float32),pltpu.VMEM((768,n),jnp.float32),pltpu.VMEM((3,S,S),BF),pltpu.VMEM((NB,3,S,S),BF),pltpu.VMEM((NB,3,S,S),BF),pltpu.VMEM((3,S,n),BF),pltpu.VMEM((768,n),BF),pltpu.VMEM((5,768,128),jnp.float32),pltpu.VMEM((768,768),jnp.float32),pltpu.VMEM((768,n),BF),pltpu.SemaphoreType.DMA((4,))],
+        compiler_params=pltpu.CompilerParams(vmem_limit_bytes=40<<20))(blocks,one,two,jnp.ones((8,128),jnp.float32))
 
 
 def body(velocity):
@@ -342,9 +367,8 @@
     share, rest = inner(velocity)
     one = lax.all_to_all(share, ("x", "c"), 0, 0, tiled=True)
     two = lax.all_to_all(outer(velocity, lo, hi, rest), ("x", "c"), 0, 0, tiled=True)
-    matrix, blocks = gram_blocks(one, two)
-    total = total_of(blocks).reshape(22, S, S)
-    factor, modes = chol_solve(total, matrix)
+    total = total_of(gram_blocks(one, two))
+    factor, modes = chol_solve(total, one, two)
     return modes.reshape(NB * S, 1, 640), factor
 
 

time: 136 us -> 132 us (0.971)
  blocking collectives: 36.2 us -> 20 us
  starting transfers between devices: 29.1 us -> 36.1 us
  waiting for transfers between devices: 32.9 us -> 39.7 us
  Pallas kernels: 32.5 us -> 30.7 us
    all_to_all x1 -> x0, blocking collectives: 15.8 us -> none  [gather_yz(): lax.all_to_all(jnp.broadcast_to(v[None], (32,) + v.shape), ('y', 'z'), 0,...]
    all_to_all x0 -> x1, waiting for transfers between devices: none -> 9.63 us  [gather_yz(): lax.all_to_all(jnp.broadcast_to(v[None], (32,) + v.shape), ('y', 'z'), 0,...]
    all_to_all x0 -> x1, starting transfers between devices: none -> 6.12 us  [gather_yz(): lax.all_to_all(jnp.broadcast_to(v[None], (32,) + v.shape), ('y', 'z'), 0,...]
    all_to_all x1, waiting for transfers between devices: 0.01 us -> 4.3 us  [body(): one = lax.all_to_all(share, ('x', 'c'), 0, 0, tiled=True)]
    ppermute x1, waiting for transfers between devices: 4.17 us -> 0.01 us  [body(): hi = lax.ppermute(velocity[:, 1:, 0:4], ('y', 'z'), backward)]
    ppermute x1, starting transfers between devices: 4.38 us -> 5.8 us  [body(): lo = lax.ppermute(velocity[:, 1:, 1:5], ('y', 'z'), forward)]
    pallas_call x1, Pallas kernels: 24.7 us -> 23.2 us  [chol_solve(): pl.pallas_call(chol_kernel, out_shape=(jax.ShapeDtypeStruct((768, 768), j...]
    all_to_all x1, starting transfers between devices: 5.95 us -> 4.57 us  [body(): lax.all_to_all(outer(velocity, lo, hi, rest), ('x', 'c'), 0, 0, tiled=True)]
  transfers between devices with their start and end apart: 12 -> 13, of which waited for: 9 -> 11; matrix products, arithmetic and copies ran while one was open for 0% -> 0% of each run, Pallas kernels for 5% -> 5%
where the time goes in v2:
time: 132 us; the launch traced here: 131 us
  waiting for transfers between devices  39.7 us (30%)
  starting transfers between devices  36.1 us (27%)
  Pallas kernels  30.7 us (23%)
  blocking collectives  20 us (15%)
  local copies, waits for them, and re-layouts  3.48 us (3%)
    pallas_call x1, Pallas kernels, chol_solve(): pl.pallas_call(chol_kernel, out_shape=(jax.ShapeDtypeStruct((768, 768), j...  23.2 us
    all_to_all x1, blocking collectives, scatter_yz(): lax.all_to_all(v.reshape(32, -1, v.shape[1]), ('y', 'z'), 0, 0, tiled=True)  20 us
    all_to_all x1, waiting for transfers between devices, body(): lax.all_to_all(outer(velocity, lo, hi, rest), ('x', 'c'), 0, 0, tiled=True)  10.8 us
    all_to_all x1, waiting for transfers between devices, gather_yz(): lax.all_to_all(jnp.broadcast_to(v[None], (32,) + v.shape), ('y', 'z'), 0,...  9.63 us
    ppermute x3, waiting for transfers between devices, scatter_x(): got.append(lax.ppermute(send, 'x', ring(4, k)))  7.32 us
    all_to_all x1, starting transfers between devices, gather_yz(): lax.all_to_all(jnp.broadcast_to(v[None], (32,) + v.shape), ('y', 'z'), 0,...  6.12 us
    all_to_all x1, starting transfers between devices, body(): one = lax.all_to_all(share, ('x', 'c'), 0, 0, tiled=True)  6.09 us
    ppermute x1, starting transfers between devices, body(): lo = lax.ppermute(velocity[:, 1:, 1:5], ('y', 'z'), forward)  5.8 us
  transfers between devices with their start and end apart: 13, of which 11 were waited for; matrix products, arithmetic and copies ran while one was open for 0% of the time, Pallas kernels for 5%

profile of v2, /device:TPU:1, one launch (start us, length us, event | category | flops | bytes accessed | tf_op | source)
XLA Modules:
  0.0 131.1 jit_solution(15412368939603775505)
XLA Ops:
  0.6 0.0 copy-start
  0.6 2.3 %fusion = (bf16[32,2,4,8,128]{4,3,2,1,0:T(8,128)(2,1)}, bf16[32,2,4,8,128]{4,3,2,1,0:T(8,128)(2,1)}) fusion(bf16[32,3,5,8,128]{4,3,2,1,0:T(8,128)(2,1)} %vel.3), kind=kLoop, calls=%fused_computation.13 | loop fusion | bytes 2097152 | tf_op jit(solution)/shard_map/slice | solution.py:366
  3.0 1.3 collective-permute-start.1
  4.3 5.8 %collective-permute-start = (bf16[32,2,4,8,128]{4,3,2,1,0:T(8,128)(2,1)}, bf16[32,2,4,8,128]{4,3,2,1,0:T(8,128)(2,1)}, u32[]{:S(2)}, u32[]{:S(2)}) collective-permute-start(bf16[32,2,4,8,128]{4,3,2,1,0:T(8,128)(2,1)} %get-tuple-element.11), channel_id=1, source_target_pairs={{0,1},{1,2},{2,3},{3,4},{4,5},{5,6},{6,7},{7,8},{8,9},{9,10},{10,1... | collective-permute-start | bytes 1572872 | tf_op jit(solution)/shard_map/ppermute | solution.py:365
  10.1 0.0 copy-done
  10.1 3.4 %shard_map.30 = (bf16[8,32,640]{2,1,0:T(8,128)(2,1)}, f32[2,32,5,8,128]{4,3,2,1,0:T(8,128)S(1)}) custom-call(bf16[32,3,5,8,128]{4,3,2,1,0:T(8,128)(2,1)S(1)} %copy-done), custom_call_target="tpu_custom_call" | custom-call | flops 10000000 | bytes 12000000 | tf_op jit(solution)/shard_map/pallas_call | solution.py:90
  13.4 6.1 %all-to-all-start = ((bf16[8,32,640]{2,1,0:T(8,128)(2,1)}), bf16[8,32,640]{2,1,0:T(8,128)(2,1)S(1)}, u32[]{:S(2)}, u32[]{:S(2)}) async-start(bf16[8,32,640]{2,1,0:T(8,128)(2,1)} %get-tuple-element.6), calls=%async_computation | async-start | bytes 655360 | tf_op jit(solution)/shard_map/all_to_all | solution.py:368
  19.5 0.0 collective-permute-done.1.hi
  19.5 0.0 collective-permute-done.lo
  19.5 2.8 %shard_map.31 = bf16[8,64,640]{2,1,0:T(8,128)(2,1)} custom-call(bf16[32,3,5,8,128]{4,3,2,1,0:T(8,128)(2,1)S(1)} %copy-done, bf16[32,2,4,8,128]{4,3,2,1,0:T(8,128)(2,1)} %collective-permute-done.lo, bf16[32,2,4,8,128]{4,3,2,1,0:T(8,128)(2,1)S(1)} %collective-permute-done.1.hi, f32[2,32,5,8,128]{4,3,2,1,0:T(8,128)S(1)} %get-tuple-element.7.rest), custom_call_target="tpu_custom_call" | custom-call | flops 10000000 | bytes 6000000 | tf_op jit(solution)/shard_map/pallas_call | solution.py:102
  22.3 4.3 %all-to-all-done.one = bf16[8,32,640]{2,1,0:T(8,128)(2,1)S(1)} async-done(((bf16[8,32,640]{2,1,0:T(8,128)(2,1)}), bf16[8,32,640]{2,1,0:T(8,128)(2,1)S(1)}, u32[]{:S(2)}, u32[]{:S(2)}) %all-to-all-start) | async-done | bytes 327712 | tf_op jit(solution)/shard_map/all_to_all | solution.py:368
  26.6 4.6 %all-to-all-start.1 = ((bf16[8,64,640]{2,1,0:T(8,128)(2,1)}), bf16[8,64,640]{2,1,0:T(8,128)(2,1)S(1)}, u32[]{:S(2)}, u32[]{:S(2)}) async-start(bf16[8,64,640]{2,1,0:T(8,128)(2,1)} %shard_map.31), calls=%async_computation.1 | async-start | bytes 1310720 | tf_op jit(solution)/shard_map/all_to_all | solution.py:369
  31.2 10.8 %all-to-all-done.1.two = bf16[8,64,640]{2,1,0:T(8,128)(2,1)S(1)} async-done(((bf16[8,64,640]{2,1,0:T(8,128)(2,1)}), bf16[8,64,640]{2,1,0:T(8,128)(2,1)S(1)}, u32[]{:S(2)}, u32[]{:S(2)}) %all-to-all-start.1) | async-done | bytes 655392 | tf_op jit(solution)/shard_map/all_to_all | solution.py:369
  42.0 1.3 shard_map.32
  43.3 1.1 collective-permute-start.2
  44.4 1.7 %collective-permute-done.2 = f32[1184,128]{1,0:T(8,128)S(1)} collective-permute-done((f32[1184,128]{1,0:T(8,128)S(1)}, f32[1184,128]{1,0:T(8,128)S(1)}, u32[]{:S(2)}, u32[]{:S(2)}) %collective-permute-start.2) | collective-permute-done | bytes 606240 | tf_op jit(solution)/shard_map/ppermute | solution.py:173
  46.0 0.1 dynamic-slice_add_fusion
  46.1 0.2 collective-permute-start.3
  46.3 2.6 %collective-permute-start.5 = (f32[296,128]{1,0:T(8,128)S(1)}, f32[296,128]{1,0:T(8,128)S(1)}, u32[]{:S(2)}, u32[]{:S(2)}) collective-permute-start(f32[296,128]{1,0:T(8,128)S(1)} %get-tuple-element.13), channel_id=1, source_target_pairs={{0,192},{64,0},{128,64},{192,128},{1,193},{65,1},{129,65},{193,129... | collective-permute-start | bytes 454664 | tf_op jit(solution)/shard_map/ppermute | solution.py:195
  48.9 0.0 collective-permute-start.4
  48.9 3.9 %collective-permute-done.3 = f32[296,128]{1,0:T(8,128)S(1)} collective-permute-done((f32[296,128]{1,0:T(8,128)S(1)}, f32[296,128]{1,0:T(8,128)S(1)}, u32[]{:S(2)}, u32[]{:S(2)}) %collective-permute-start.3) | collective-permute-done | bytes 151584 | tf_op jit(solution)/shard_map/ppermute | solution.py:195
  52.8 1.7 %collective-permute-done.5 = f32[296,128]{1,0:T(8,128)S(1)} collective-permute-done((f32[296,128]{1,0:T(8,128)S(1)}, f32[296,128]{1,0:T(8,128)S(1)}, u32[]{:S(2)}, u32[]{:S(2)}) %collective-permute-start.5) | collective-permute-done | bytes 151584 | tf_op jit(solution)/shard_map/ppermute | solution.py:195
  54.6 1.7 %collective-permute-done.4 = f32[296,128]{1,0:T(8,128)S(1)} collective-permute-done((f32[296,128]{1,0:T(8,128)S(1)}, f32[296,128]{1,0:T(8,128)S(1)}, u32[]{:S(2)}, u32[]{:S(2)}) %collective-permute-start.4) | collective-permute-done | bytes 151584 | tf_op jit(solution)/shard_map/ppermute | solution.py:195
  56.3 20.0 %all_to_all.20 = f32[32,10,128]{2,1,0:T(8,128)S(1)} all-to-all(f32[32,10,128]{2,1,0:T(8,128)S(1)} %reshape.16), channel_id=1, replica_groups=mesh['x'=4,'c'=2,'y'=4,'z'=8] {'y','z'}, dimensions={0} | all-to-all | bytes 327680 | tf_op jit(solution)/shard_map/all_to_all | solution.py:215
  76.4 0.7 broadcast_in_dim.17
  77.1 6.1 %all-to-all-start.3 = ((f32[32,10,128]{2,1,0:T(8,128)}), f32[32,10,128]{2,1,0:T(8,128)S(1)}, u32[]{:S(2)}, u32[]{:S(2)}) async-start(f32[32,10,128]{2,1,0:T(8,128)} %broadcast_in_dim.17), calls=%async_computation.3 | async-start | bytes 524288 | tf_op jit(solution)/shard_map/all_to_all | solution.py:220
  83.3 9.6 %all-to-all-done.3 = f32[32,10,128]{2,1,0:T(8,128)S(1)} async-done(((f32[32,10,128]{2,1,0:T(8,128)}), f32[32,10,128]{2,1,0:T(8,128)S(1)}, u32[]{:S(2)}, u32[]{:S(2)}) %all-to-all-start.3) | async-done | bytes 163872 | tf_op jit(solution)/shard_map/all_to_all | solution.py:220
  93.0 0.4 collective-permute-start.6
  93.4 2.7 %collective-permute-start.7 = (f32[296,128]{1,0:T(8,128)S(1)}, f32[296,128]{1,0:T(8,128)S(1)}, u32[]{:S(2)}, u32[]{:S(2)}) collective-permute-start(f32[296,128]{1,0:T(8,128)S(1)} %get-tuple-element.15), channel_id=1, source_target_pairs={{0,128},{64,192},{128,0},{192,64},{1,129},{65,193},{129,1},{193,65... | collective-permute-start | bytes 454664 | tf_op jit(solution)/shard_map/ppermute | solution.py:206
  96.0 0.0 collective-permute-start.8
  96.1 2.3 %collective-permute-done.6 = f32[296,128]{1,0:T(8,128)S(1)} collective-permute-done((f32[296,128]{1,0:T(8,128)S(1)}, f32[296,128]{1,0:T(8,128)S(1)}, u32[]{:S(2)}, u32[]{:S(2)}) %collective-permute-start.6) | collective-permute-done | bytes 151584 | tf_op jit(solution)/shard_map/ppermute | solution.py:206
  98.3 1.9 %collective-permute-done.7 = f32[296,128]{1,0:T(8,128)S(1)} collective-permute-done((f32[296,128]{1,0:T(8,128)S(1)}, f32[296,128]{1,0:T(8,128)S(1)}, u32[]{:S(2)}, u32[]{:S(2)}) %collective-permute-start.7) | collective-permute-done | bytes 151584 | tf_op jit(solution)/shard_map/ppermute | solution.py:206
  100.3 0.3 collective-permute-done.8
  100.6 5.4 %collective-permute-start.9 = (f32[1184,128]{1,0:T(8,128)S(1)}, f32[1184,128]{1,0:T(8,128)S(1)}, u32[]{:S(2)}, u32[]{:S(2)}) collective-permute-start(f32[1184,128]{1,0:T(8,128)S(1)} %constant_dynamic-update-slice_fusion.2), channel_id=1, source_target_pairs={{0,32},{32,0},{1,33},{33,1},{2,34},{34,2},{3,35},{35,3},{4,36},{36... | collective-permute-start | bytes 1818632 | tf_op jit(solution)/shard_map/ppermute | solution.py:179
  105.9 0.1 broadcast_in_dim.15
  106.0 1.5 %collective-permute-done.9 = f32[1184,128]{1,0:T(8,128)S(1)} collective-permute-done((f32[1184,128]{1,0:T(8,128)S(1)}, f32[1184,128]{1,0:T(8,128)S(1)}, u32[]{:S(2)}, u32[]{:S(2)}) %collective-permute-start.9) | collective-permute-done | bytes 606240 | tf_op jit(solution)/shard_map/ppermute | solution.py:179
  107.6 23.2 %shard_map.33 = (f32[768,768]{1,0:T(8,128)}, bf16[768,640]{1,0:T(8,128)(2,1)}) custom-call(f32[2368,128]{1,0:T(8,128)S(1)} %constant_dynamic-update-slice_fusion.a_ref, bf16[8,32,640]{2,1,0:T(8,128)(2,1)S(1)} %all-to-all-done.one, bf16[8,64,640]{2,1,0:T(8,128)(2,1)S(1)} %all-to-all-done.1.two, f32[8,128]{1,0:T(8,128)S(1)} %broadcast_in_dim.18.ones), custom_call_target="tpu_custom_call" | custom-call | tf_op jit(solution)/shard_map/pallas_call | solution.py:355
  (16 shorter events, 0.4 us)
Async XLA Ops:
  0.6 9.4 %copy-start = (bf16[32,3,5,8,128]{4,3,2,1,0:T(8,128)(2,1)S(1)}, bf16[32,3,5,8,128]{4,3,2,1,0:T(8,128)(2,1)}, u32[]{:S(2)}) copy-start(bf16[32,3,5,8,128]{4,3,2,1,0:T(8,128)(2,1)} %vel.3) | copy-start | bytes 2949124
  3.0 16.5 %collective-permute-start.1 = (bf16[32,2,4,8,128]{4,3,2,1,0:T(8,128)(2,1)}, bf16[32,2,4,8,128]{4,3,2,1,0:T(8,128)(2,1)S(1)}, u32[]{:S(2)}, u32[]{:S(2)}) collective-permute-start(bf16[32,2,4,8,128]{4,3,2,1,0:T(8,128)(2,1)} %get-tuple-element.10), channel_id=1, source_target_pairs={{1,0},{2,1},{3,2},{4,3},{5,4},{6,5},{7,6},{8,7},{9,8},{10,9},{11,1... | collective-permute-start | bytes 1572872 | tf_op jit(solution)/shard_map/ppermute | solution.py:366
  4.3 15.3 %collective-permute-start = (bf16[32,2,4,8,128]{4,3,2,1,0:T(8,128)(2,1)}, bf16[32,2,4,8,128]{4,3,2,1,0:T(8,128)(2,1)}, u32[]{:S(2)}, u32[]{:S(2)}) collective-permute-start(bf16[32,2,4,8,128]{4,3,2,1,0:T(8,128)(2,1)} %get-tuple-element.11), channel_id=1, source_target_pairs={{0,1},{1,2},{2,3},{3,4},{4,5},{5,6},{6,7},{7,8},{8,9},{9,10},{10,1... | collective-permute-start | bytes 1572872 | tf_op jit(solution)/shard_map/ppermute | solution.py:365
  13.4 13.2 %all-to-all-start = ((bf16[8,32,640]{2,1,0:T(8,128)(2,1)}), bf16[8,32,640]{2,1,0:T(8,128)(2,1)S(1)}, u32[]{:S(2)}, u32[]{:S(2)}) async-start(bf16[8,32,640]{2,1,0:T(8,128)(2,1)} %get-tuple-element.6), calls=%async_computation | async-start | bytes 655360 | tf_op jit(solution)/shard_map/all_to_all | solution.py:368
  26.6 15.4 %all-to-all-start.1 = ((bf16[8,64,640]{2,1,0:T(8,128)(2,1)}), bf16[8,64,640]{2,1,0:T(8,128)(2,1)S(1)}, u32[]{:S(2)}, u32[]{:S(2)}) async-start(bf16[8,64,640]{2,1,0:T(8,128)(2,1)} %shard_map.31), calls=%async_computation.1 | async-start | bytes 1310720 | tf_op jit(solution)/shard_map/all_to_all | solution.py:369
  43.3 2.7 %collective-permute-start.2 = (f32[1184,128]{1,0:T(8,128)S(1)}, f32[1184,128]{1,0:T(8,128)S(1)}, u32[]{:S(2)}, u32[]{:S(2)}) collective-permute-start(f32[1184,128]{1,0:T(8,128)S(1)} %constant_dynamic-slice_fusion.3), channel_id=1, source_target_pairs={{0,32},{32,0},{1,33},{33,1},{2,34},{34,2},{3,35},{35,3},{4,36},{36... | collective-permute-start | bytes 1818632 | tf_op jit(solution)/shard_map/ppermute | solution.py:173
  46.1 6.7 %collective-permute-start.3 = (f32[296,128]{1,0:T(8,128)S(1)}, f32[296,128]{1,0:T(8,128)S(1)}, u32[]{:S(2)}, u32[]{:S(2)}) collective-permute-start(f32[296,128]{1,0:T(8,128)S(1)} %get-tuple-element.12), channel_id=1, source_target_pairs={{0,128},{64,192},{128,0},{192,64},{1,129},{65,193},{129,1},{193,65... | collective-permute-start | bytes 454664 | tf_op jit(solution)/shard_map/ppermute | solution.py:195
  46.3 8.3 %collective-permute-start.5 = (f32[296,128]{1,0:T(8,128)S(1)}, f32[296,128]{1,0:T(8,128)S(1)}, u32[]{:S(2)}, u32[]{:S(2)}) collective-permute-start(f32[296,128]{1,0:T(8,128)S(1)} %get-tuple-element.13), channel_id=1, source_target_pairs={{0,192},{64,0},{128,64},{192,128},{1,193},{65,1},{129,65},{193,129... | collective-permute-start | bytes 454664 | tf_op jit(solution)/shard_map/ppermute | solution.py:195
  48.9 7.3 %collective-permute-start.4 = (f32[296,128]{1,0:T(8,128)S(1)}, f32[296,128]{1,0:T(8,128)S(1)}, u32[]{:S(2)}, u32[]{:S(2)}) collective-permute-start(f32[296,128]{1,0:T(8,128)S(1)} %get-tuple-element.14), channel_id=1, source_target_pairs={{0,64},{64,128},{128,192},{192,0},{1,65},{65,129},{129,193},{193,1... | collective-permute-start | bytes 454664 | tf_op jit(solution)/shard_map/ppermute | solution.py:195
  77.1 15.8 %all-to-all-start.3 = ((f32[32,10,128]{2,1,0:T(8,128)}), f32[32,10,128]{2,1,0:T(8,128)S(1)}, u32[]{:S(2)}, u32[]{:S(2)}) async-start(f32[32,10,128]{2,1,0:T(8,128)} %broadcast_in_dim.17), calls=%async_computation.3 | async-start | bytes 524288 | tf_op jit(solution)/shard_map/all_to_all | solution.py:220
  93.0 5.3 %collective-permute-start.6 = (f32[296,128]{1,0:T(8,128)S(1)}, f32[296,128]{1,0:T(8,128)S(1)}, u32[]{:S(2)}, u32[]{:S(2)}) collective-permute-start(f32[296,128]{1,0:T(8,128)S(1)} %get-tuple-element.15), channel_id=1, source_target_pairs={{0,64},{64,128},{128,192},{192,0},{1,65},{65,129},{129,193},{193,1... | collective-permute-start | bytes 454664 | tf_op jit(solution)/shard_map/ppermute | solution.py:206
  93.4 6.9 %collective-permute-start.7 = (f32[296,128]{1,0:T(8,128)S(1)}, f32[296,128]{1,0:T(8,128)S(1)}, u32[]{:S(2)}, u32[]{:S(2)}) collective-permute-start(f32[296,128]{1,0:T(8,128)S(1)} %get-tuple-element.15), channel_id=1, source_target_pairs={{0,128},{64,192},{128,0},{192,64},{1,129},{65,193},{129,1},{193,65... | collective-permute-start | bytes 454664 | tf_op jit(solution)/shard_map/ppermute | solution.py:206
  96.0 4.5 %collective-permute-start.8 = (f32[296,128]{1,0:T(8,128)S(1)}, f32[296,128]{1,0:T(8,128)S(1)}, u32[]{:S(2)}, u32[]{:S(2)}) collective-permute-start(f32[296,128]{1,0:T(8,128)S(1)} %get-tuple-element.15), channel_id=1, source_target_pairs={{0,192},{64,0},{128,64},{192,128},{1,193},{65,1},{129,65},{193,129... | collective-permute-start | bytes 454664 | tf_op jit(solution)/shard_map/ppermute | solution.py:206
  100.6 7.0 %collective-permute-start.9 = (f32[1184,128]{1,0:T(8,128)S(1)}, f32[1184,128]{1,0:T(8,128)S(1)}, u32[]{:S(2)}, u32[]{:S(2)}) collective-permute-start(f32[1184,128]{1,0:T(8,128)S(1)} %constant_dynamic-update-slice_fusion.2), channel_id=1, source_target_pairs={{0,32},{32,0},{1,33},{33,1},{2,34},{34,2},{3,35},{35,3},{4,36},{36... | collective-permute-start | bytes 1818632 | tf_op jit(solution)/shard_map/ppermute | solution.py:179

commit v3 on v2

--- a/solution.py
+++ b/solution.py
@@ -185,45 +185,45 @@
     return [(j, (j + k) % n) for j in range(n)]
 
 
-def scatter_x(v):
-    i = lax.axis_index("x")
+def scatter_ring(v, axis):
+    i = lax.axis_index(axis)
     h = v.shape[0] // 4
     total = lax.dynamic_slice_in_dim(v, i * h, h, 0)
     got = []
     for k in (2, 1, 3):
         send = lax.dynamic_slice_in_dim(v, ((i + k) % 4) * h, h, 0)
-        got.append(lax.ppermute(send, "x", ring(4, k)))
+        got.append(lax.ppermute(send, axis, ring(4, k)))
     for g in got:
         total = total + g
     return total
 
 
-def gather_x(v):
-    i = lax.axis_index("x")
+def gather_ring(v, axis):
+    i = lax.axis_index(axis)
     h = v.shape[0]
     parts = {0: v}
     for k in (2, 1, 3):
-        parts[k] = lax.ppermute(v, "x", ring(4, k))
+        parts[k] = lax.ppermute(v, axis, ring(4, k))
     out = jnp.zeros((4 * h,) + v.shape[1:], v.dtype)
     for k in range(4):
         out = lax.dynamic_update_slice_in_dim(out, parts[k], ((i - k) % 4) * h, 0)
     return out
 
 
-def scatter_yz(v):
-    v = jnp.pad(v, ((0, 320 - SHARE), (0, 0)))
-    got = lax.all_to_all(v.reshape(32, -1, v.shape[1]), ("y", "z"), 0, 0, tiled=True)
-    return got.sum(0)
-
-
-def gather_yz(v):
-    got = lax.all_to_all(jnp.broadcast_to(v[None], (32,) + v.shape), ("y", "z"), 0, 0, tiled=True)
-    return got.reshape(-1, v.shape[1])[:SHARE]
+def scatter_z(v):
+    return lax.all_to_all(v.reshape(8, -1, v.shape[1]), "z", 0, 0, tiled=True).sum(0)
+
+
+def gather_z(v):
+    got = lax.all_to_all(jnp.broadcast_to(v[None], (8,) + v.shape), "z", 0, 0, tiled=True)
+    return got.reshape(-1, v.shape[1])
 
 
 def total_of(v):
-    share = scatter_yz(scatter_x(scatter_core(v))) / POINTS
-    return gather_core(gather_x(gather_yz(share)))
+    share = scatter_ring(scatter_core(v), "x")
+    share = scatter_ring(jnp.pad(share, ((0, 320 - SHARE), (0, 0))), "y")
+    share = lax.all_to_all(jnp.broadcast_to(share[None], (8,) + share.shape), "z", 0, 0, tiled=True).sum(0) / POINTS
+    return gather_core(gather_ring(gather_ring(share, "y")[:SHARE], "x"))
 
 
 BF=jnp.bfloat16

time: 132 us -> 131 us (level)
  blocking collectives: 20 us -> 0 us
  starting transfers between devices: 36.1 us -> 51.3 us
  waiting for transfers between devices: 39.7 us -> 43.8 us
    all_to_all x1 -> x0, blocking collectives: 20 us -> none  [scatter_yz(): lax.all_to_all(v.reshape(32, -1, v.shape[1]), ('y', 'z'), 0, 0, tiled=True)]
    ppermute x6 -> x12, starting transfers between devices: 5.84 us -> 21.7 us  [the longest x6 14.1 us: scatter_ring(): got.append(lax.ppermute(send, axis, ring(4, k)))]
    ppermute x6 -> x12, waiting for transfers between devices: 11.8 us -> 15.6 us  [the longest x6 8.71 us: scatter_ring(): got.append(lax.ppermute(send, axis, ring(4, k)))]
    all_to_all x1, starting transfers between devices: 6.12 us -> 3.43 us  [total_of(): lax.all_to_all(jnp.broadcast_to(share[None], (8,) + share.shape), 'z', 0,...]
    ppermute x1, starting transfers between devices: 5.35 us -> 7.4 us  [gather_core(): o = lax.ppermute(v, 'c', SWAP)]
  transfers between devices with their start and end apart: 13 -> 19, of which waited for: 11 -> 14; matrix products, arithmetic and copies ran while one was open for 0% -> 0% of each run, Pallas kernels for 5% -> 5%
where the time goes in v3:
time: 131 us
  starting transfers between devices  51.3 us (39%)
  waiting for transfers between devices  43.8 us (33%)
  Pallas kernels  30.7 us (23%)
  local copies, waits for them, and re-layouts  3.51 us (3%)
    pallas_call x1, Pallas kernels, chol_solve(): pl.pallas_call(chol_kernel, out_shape=(jax.ShapeDtypeStruct((768, 768), j...  23.2 us
    ppermute x6, starting transfers between devices, scatter_ring(): got.append(lax.ppermute(send, axis, ring(4, k)))  14.1 us
    all_to_all x1, waiting for transfers between devices, body(): lax.all_to_all(outer(velocity, lo, hi, rest), ('x', 'c'), 0, 0, tiled=True)  10.8 us
    all_to_all x1, waiting for transfers between devices, total_of(): lax.all_to_all(jnp.broadcast_to(share[None], (8,) + share.shape), 'z', 0,...  9.86 us
    ppermute x6, waiting for transfers between devices, scatter_ring(): got.append(lax.ppermute(send, axis, ring(4, k)))  8.71 us
    ppermute x6, starting transfers between devices, gather_ring(): parts[k] = lax.ppermute(v, axis, ring(4, k))  7.57 us
    ppermute x1, starting transfers between devices, gather_core(): o = lax.ppermute(v, 'c', SWAP)  7.4 us
    ppermute x6, waiting for transfers between devices, gather_ring(): parts[k] = lax.ppermute(v, axis, ring(4, k))  6.94 us
  transfers between devices with their start and end apart: 19, of which 14 were waited for; matrix products, arithmetic and copies ran while one was open for 0% of the time, Pallas kernels for 5%

profile of v3, /device:TPU:1, one launch (start us, length us, event | category | flops | bytes accessed | tf_op | source)
XLA Modules:
  0.0 130.5 jit_solution(2128413734986548869)
XLA Ops:
  0.6 0.0 copy-start
  0.6 2.3 %fusion.3 = (bf16[32,2,4,8,128]{4,3,2,1,0:T(8,128)(2,1)}, bf16[32,2,4,8,128]{4,3,2,1,0:T(8,128)(2,1)}) fusion(bf16[32,3,5,8,128]{4,3,2,1,0:T(8,128)(2,1)} %vel.3), kind=kLoop, calls=%fused_computation.24 | loop fusion | bytes 2097152 | tf_op jit(solution)/shard_map/slice | solution.py:366
  3.0 1.3 collective-permute-start.1
  4.3 5.8 %collective-permute-start = (bf16[32,2,4,8,128]{4,3,2,1,0:T(8,128)(2,1)}, bf16[32,2,4,8,128]{4,3,2,1,0:T(8,128)(2,1)}, u32[]{:S(2)}, u32[]{:S(2)}) collective-permute-start(bf16[32,2,4,8,128]{4,3,2,1,0:T(8,128)(2,1)} %get-tuple-element.11), channel_id=1, source_target_pairs={{0,1},{1,2},{2,3},{3,4},{4,5},{5,6},{6,7},{7,8},{8,9},{9,10},{10,1... | collective-permute-start | bytes 1572872 | tf_op jit(solution)/shard_map/ppermute | solution.py:365
  10.1 0.0 copy-done
  10.1 3.4 %shard_map.30 = (bf16[8,32,640]{2,1,0:T(8,128)(2,1)}, f32[2,32,5,8,128]{4,3,2,1,0:T(8,128)S(1)}) custom-call(bf16[32,3,5,8,128]{4,3,2,1,0:T(8,128)(2,1)S(1)} %copy-done), custom_call_target="tpu_custom_call" | custom-call | flops 10000000 | bytes 12000000 | tf_op jit(solution)/shard_map/pallas_call | solution.py:90
  13.5 6.1 %all-to-all-start = ((bf16[8,32,640]{2,1,0:T(8,128)(2,1)}), bf16[8,32,640]{2,1,0:T(8,128)(2,1)S(1)}, u32[]{:S(2)}, u32[]{:S(2)}) async-start(bf16[8,32,640]{2,1,0:T(8,128)(2,1)} %get-tuple-element.6), calls=%async_computation | async-start | bytes 655360 | tf_op jit(solution)/shard_map/all_to_all | solution.py:368
  19.6 0.0 collective-permute-done.1.hi
  19.6 0.0 collective-permute-done.lo
  19.6 2.8 %shard_map.31 = bf16[8,64,640]{2,1,0:T(8,128)(2,1)} custom-call(bf16[32,3,5,8,128]{4,3,2,1,0:T(8,128)(2,1)S(1)} %copy-done, bf16[32,2,4,8,128]{4,3,2,1,0:T(8,128)(2,1)} %collective-permute-done.lo, bf16[32,2,4,8,128]{4,3,2,1,0:T(8,128)(2,1)S(1)} %collective-permute-done.1.hi, f32[2,32,5,8,128]{4,3,2,1,0:T(8,128)S(1)} %get-tuple-element.7.rest), custom_call_target="tpu_custom_call" | custom-call | flops 10000000 | bytes 6000000 | tf_op jit(solution)/shard_map/pallas_call | solution.py:102
  22.4 4.3 %all-to-all-done.one = bf16[8,32,640]{2,1,0:T(8,128)(2,1)S(1)} async-done(((bf16[8,32,640]{2,1,0:T(8,128)(2,1)}), bf16[8,32,640]{2,1,0:T(8,128)(2,1)S(1)}, u32[]{:S(2)}, u32[]{:S(2)}) %all-to-all-start) | async-done | bytes 327712 | tf_op jit(solution)/shard_map/all_to_all | solution.py:368
  26.7 4.6 %all-to-all-start.1 = ((bf16[8,64,640]{2,1,0:T(8,128)(2,1)}), bf16[8,64,640]{2,1,0:T(8,128)(2,1)S(1)}, u32[]{:S(2)}, u32[]{:S(2)}) async-start(bf16[8,64,640]{2,1,0:T(8,128)(2,1)} %shard_map.31), calls=%async_computation.1 | async-start | bytes 1310720 | tf_op jit(solution)/shard_map/all_to_all | solution.py:369
  31.2 10.8 %all-to-all-done.1.two = bf16[8,64,640]{2,1,0:T(8,128)(2,1)S(1)} async-done(((bf16[8,64,640]{2,1,0:T(8,128)(2,1)}), bf16[8,64,640]{2,1,0:T(8,128)(2,1)S(1)}, u32[]{:S(2)}, u32[]{:S(2)}) %all-to-all-start.1) | async-done | bytes 655392 | tf_op jit(solution)/shard_map/all_to_all | solution.py:369
  42.0 1.3 shard_map.32
  43.3 1.1 collective-permute-start.2
  44.4 1.7 %collective-permute-done.2 = f32[1184,128]{1,0:T(8,128)S(1)} collective-permute-done((f32[1184,128]{1,0:T(8,128)S(1)}, f32[1184,128]{1,0:T(8,128)S(1)}, u32[]{:S(2)}, u32[]{:S(2)}) %collective-permute-start.2) | collective-permute-done | bytes 606240 | tf_op jit(solution)/shard_map/ppermute | solution.py:173
  46.1 0.1 dynamic-slice_add_fusion
  46.2 0.2 collective-permute-start.3
  46.3 2.6 %collective-permute-start.5 = (f32[296,128]{1,0:T(8,128)S(1)}, f32[296,128]{1,0:T(8,128)S(1)}, u32[]{:S(2)}, u32[]{:S(2)}) collective-permute-start(f32[296,128]{1,0:T(8,128)S(1)} %get-tuple-element.13), channel_id=1, source_target_pairs={{0,192},{64,0},{128,64},{192,128},{1,193},{65,1},{129,65},{193,129... | collective-permute-start | bytes 454664 | tf_op jit(solution)/shard_map/ppermute | solution.py:195
  48.9 0.0 collective-permute-start.4
  49.0 3.9 %collective-permute-done.3 = f32[296,128]{1,0:T(8,128)S(1)} collective-permute-done((f32[296,128]{1,0:T(8,128)S(1)}, f32[296,128]{1,0:T(8,128)S(1)}, u32[]{:S(2)}, u32[]{:S(2)}) %collective-permute-start.3) | collective-permute-done | bytes 151584 | tf_op jit(solution)/shard_map/ppermute | solution.py:195
  52.9 1.7 %collective-permute-done.5 = f32[296,128]{1,0:T(8,128)S(1)} collective-permute-done((f32[296,128]{1,0:T(8,128)S(1)}, f32[296,128]{1,0:T(8,128)S(1)}, u32[]{:S(2)}, u32[]{:S(2)}) %collective-permute-start.5) | collective-permute-done | bytes 151584 | tf_op jit(solution)/shard_map/ppermute | solution.py:195
  54.6 1.7 %collective-permute-done.4 = f32[296,128]{1,0:T(8,128)S(1)} collective-permute-done((f32[296,128]{1,0:T(8,128)S(1)}, f32[296,128]{1,0:T(8,128)S(1)}, u32[]{:S(2)}, u32[]{:S(2)}) %collective-permute-start.4) | collective-permute-done | bytes 151584 | tf_op jit(solution)/shard_map/ppermute | solution.py:195
  56.4 8.7 %collective-permute-start.6 = (f32[80,128]{1,0:T(8,128)S(1)}, f32[80,128]{1,0:T(8,128)S(1)}, u32[]{:S(2)}, u32[]{:S(2)}) collective-permute-start(f32[80,128]{1,0:T(8,128)S(1)} %get-tuple-element.17), channel_id=1, source_target_pairs={{0,16},{8,24},{16,0},{24,8},{1,17},{9,25},{17,1},{25,9},{2,18},{10... | collective-permute-start | bytes 122888 | tf_op jit(solution)/shard_map/ppermute | solution.py:195
  65.0 0.7 collective-permute-start.7
  65.7 2.0 %collective-permute-start.8 = (f32[80,128]{1,0:T(8,128)S(1)}, f32[80,128]{1,0:T(8,128)S(1)}, u32[]{:S(2)}, u32[]{:S(2)}) collective-permute-start(f32[80,128]{1,0:T(8,128)S(1)} %get-tuple-element.19), channel_id=1, source_target_pairs={{0,24},{8,0},{16,8},{24,16},{1,25},{9,1},{17,9},{25,17},{2,26},{10... | collective-permute-start | bytes 122888 | tf_op jit(solution)/shard_map/ppermute | solution.py:195
  67.7 0.0 collective-permute-done.6
  67.7 1.4 %collective-permute-done.7 = f32[80,128]{1,0:T(8,128)S(1)} collective-permute-done((f32[80,128]{1,0:T(8,128)S(1)}, f32[80,128]{1,0:T(8,128)S(1)}, u32[]{:S(2)}, u32[]{:S(2)}) %collective-permute-start.7) | collective-permute-done | bytes 40992 | tf_op jit(solution)/shard_map/ppermute | solution.py:195
  69.1 0.0 collective-permute-done.8
  69.1 0.7 broadcast_in_dim.21
  69.8 3.4 %all-to-all-start.2 = ((f32[8,80,128]{2,1,0:T(8,128)}), f32[8,80,128]{2,1,0:T(8,128)S(1)}, u32[]{:S(2)}, u32[]{:S(2)}) async-start(f32[8,80,128]{2,1,0:T(8,128)} %broadcast_in_dim.21), calls=%async_computation.2 | async-start | bytes 655360 | tf_op jit(solution)/shard_map/all_to_all | solution.py:225
  73.3 9.9 %all-to-all-done.2 = f32[8,80,128]{2,1,0:T(8,128)S(1)} async-done(((f32[8,80,128]{2,1,0:T(8,128)}), f32[8,80,128]{2,1,0:T(8,128)S(1)}, u32[]{:S(2)}, u32[]{:S(2)}) %all-to-all-start.2) | async-done | bytes 327712 | tf_op jit(solution)/shard_map/all_to_all | solution.py:225
  83.2 0.1 collective-permute-start.9
  83.4 4.1 %collective-permute-start.10 = (f32[80,128]{1,0:T(8,128)S(1)}, f32[80,128]{1,0:T(8,128)S(1)}, u32[]{:S(2)}, u32[]{:S(2)}) collective-permute-start(f32[80,128]{1,0:T(8,128)S(1)} %get-tuple-element.20), channel_id=1, source_target_pairs={{0,16},{8,24},{16,0},{24,8},{1,17},{9,25},{17,1},{25,9},{2,18},{10... | collective-permute-start | bytes 122888 | tf_op jit(solution)/shard_map/ppermute | solution.py:206
  87.5 0.4 collective-permute-start.11
  87.9 0.0 collective-permute-done.9
  87.9 1.4 %collective-permute-done.10 = f32[80,128]{1,0:T(8,128)S(1)} collective-permute-done((f32[80,128]{1,0:T(8,128)S(1)}, f32[80,128]{1,0:T(8,128)S(1)}, u32[]{:S(2)}, u32[]{:S(2)}) %collective-permute-start.10) | collective-permute-done | bytes 40992 | tf_op jit(solution)/shard_map/ppermute | solution.py:206
  89.3 1.0 collective-permute-done.11
  90.4 0.1 collective-permute-start.12
  90.5 2.9 %collective-permute-start.13 = (f32[296,128]{1,0:T(8,128)S(1)}, f32[296,128]{1,0:T(8,128)S(1)}, u32[]{:S(2)}, u32[]{:S(2)}) collective-permute-start(f32[296,128]{1,0:T(8,128)S(1)} %get-tuple-element.15), channel_id=1, source_target_pairs={{0,128},{64,192},{128,0},{192,64},{1,129},{65,193},{129,1},{193,65... | collective-permute-start | bytes 454664 | tf_op jit(solution)/shard_map/ppermute | solution.py:206
  93.4 0.0 collective-permute-start.14
  93.4 2.3 %collective-permute-done.12 = f32[296,128]{1,0:T(8,128)S(1)} collective-permute-done((f32[296,128]{1,0:T(8,128)S(1)}, f32[296,128]{1,0:T(8,128)S(1)}, u32[]{:S(2)}, u32[]{:S(2)}) %collective-permute-start.12) | collective-permute-done | bytes 151584 | tf_op jit(solution)/shard_map/ppermute | solution.py:206
  95.8 1.8 %collective-permute-done.13 = f32[296,128]{1,0:T(8,128)S(1)} collective-permute-done((f32[296,128]{1,0:T(8,128)S(1)}, f32[296,128]{1,0:T(8,128)S(1)}, u32[]{:S(2)}, u32[]{:S(2)}) %collective-permute-start.13) | collective-permute-done | bytes 151584 | tf_op jit(solution)/shard_map/ppermute | solution.py:206
  97.6 0.4 collective-permute-done.14
  98.0 7.4 %collective-permute-start.15 = (f32[1184,128]{1,0:T(8,128)S(1)}, f32[1184,128]{1,0:T(8,128)S(1)}, u32[]{:S(2)}, u32[]{:S(2)}) collective-permute-start(f32[1184,128]{1,0:T(8,128)S(1)} %constant_dynamic-update-slice_fusion.2), channel_id=1, source_target_pairs={{0,32},{32,0},{1,33},{33,1},{2,34},{34,2},{3,35},{35,3},{4,36},{36... | collective-permute-start | bytes 1818632 | tf_op jit(solution)/shard_map/ppermute | solution.py:179
  105.4 0.1 broadcast_in_dim.18
  105.5 1.5 %collective-permute-done.15 = f32[1184,128]{1,0:T(8,128)S(1)} collective-permute-done((f32[1184,128]{1,0:T(8,128)S(1)}, f32[1184,128]{1,0:T(8,128)S(1)}, u32[]{:S(2)}, u32[]{:S(2)}) %collective-permute-start.15) | collective-permute-done | bytes 606240 | tf_op jit(solution)/shard_map/ppermute | solution.py:179
  107.1 23.2 %shard_map.33 = (f32[768,768]{1,0:T(8,128)}, bf16[768,640]{1,0:T(8,128)(2,1)}) custom-call(f32[2368,128]{1,0:T(8,128)S(1)} %constant_dynamic-update-slice_fusion.a_ref, bf16[8,32,640]{2,1,0:T(8,128)(2,1)S(1)} %all-to-all-done.one, bf16[8,64,640]{2,1,0:T(8,128)(2,1)S(1)} %all-to-all-done.1.two, f32[8,128]{1,0:T(8,128)S(1)} %broadcast_in_dim.22.ones), custom_call_target="tpu_custom_call" | custom-call | tf_op jit(solution)/shard_map/pallas_call | solution.py:355
  (19 shorter events, 0.4 us)
Async XLA Ops:
  0.6 9.4 %copy-start = (bf16[32,3,5,8,128]{4,3,2,1,0:T(8,128)(2,1)S(1)}, bf16[32,3,5,8,128]{4,3,2,1,0:T(8,128)(2,1)}, u32[]{:S(2)}) copy-start(bf16[32,3,5,8,128]{4,3,2,1,0:T(8,128)(2,1)} %vel.3) | copy-start | bytes 2949124
  3.0 16.6 %collective-permute-start.1 = (bf16[32,2,4,8,128]{4,3,2,1,0:T(8,128)(2,1)}, bf16[32,2,4,8,128]{4,3,2,1,0:T(8,128)(2,1)S(1)}, u32[]{:S(2)}, u32[]{:S(2)}) collective-permute-start(bf16[32,2,4,8,128]{4,3,2,1,0:T(8,128)(2,1)} %get-tuple-element.10), channel_id=1, source_target_pairs={{1,0},{2,1},{3,2},{4,3},{5,4},{6,5},{7,6},{8,7},{9,8},{10,9},{11,1... | collective-permute-start | bytes 1572872 | tf_op jit(solution)/shard_map/ppermute | solution.py:366
  4.3 15.3 %collective-permute-start = (bf16[32,2,4,8,128]{4,3,2,1,0:T(8,128)(2,1)}, bf16[32,2,4,8,128]{4,3,2,1,0:T(8,128)(2,1)}, u32[]{:S(2)}, u32[]{:S(2)}) collective-permute-start(bf16[32,2,4,8,128]{4,3,2,1,0:T(8,128)(2,1)} %get-tuple-element.11), channel_id=1, source_target_pairs={{0,1},{1,2},{2,3},{3,4},{4,5},{5,6},{6,7},{7,8},{8,9},{9,10},{10,1... | collective-permute-start | bytes 1572872 | tf_op jit(solution)/shard_map/ppermute | solution.py:365
  13.5 13.2 %all-to-all-start = ((bf16[8,32,640]{2,1,0:T(8,128)(2,1)}), bf16[8,32,640]{2,1,0:T(8,128)(2,1)S(1)}, u32[]{:S(2)}, u32[]{:S(2)}) async-start(bf16[8,32,640]{2,1,0:T(8,128)(2,1)} %get-tuple-element.6), calls=%async_computation | async-start | bytes 655360 | tf_op jit(solution)/shard_map/all_to_all | solution.py:368
  26.7 15.4 %all-to-all-start.1 = ((bf16[8,64,640]{2,1,0:T(8,128)(2,1)}), bf16[8,64,640]{2,1,0:T(8,128)(2,1)S(1)}, u32[]{:S(2)}, u32[]{:S(2)}) async-start(bf16[8,64,640]{2,1,0:T(8,128)(2,1)} %shard_map.31), calls=%async_computation.1 | async-start | bytes 1310720 | tf_op jit(solution)/shard_map/all_to_all | solution.py:369
  43.3 2.7 %collective-permute-start.2 = (f32[1184,128]{1,0:T(8,128)S(1)}, f32[1184,128]{1,0:T(8,128)S(1)}, u32[]{:S(2)}, u32[]{:S(2)}) collective-permute-start(f32[1184,128]{1,0:T(8,128)S(1)} %constant_dynamic-slice_fusion.3), channel_id=1, source_target_pairs={{0,32},{32,0},{1,33},{33,1},{2,34},{34,2},{3,35},{35,3},{4,36},{36... | collective-permute-start | bytes 1818632 | tf_op jit(solution)/shard_map/ppermute | solution.py:173
  46.2 6.7 %collective-permute-start.3 = (f32[296,128]{1,0:T(8,128)S(1)}, f32[296,128]{1,0:T(8,128)S(1)}, u32[]{:S(2)}, u32[]{:S(2)}) collective-permute-start(f32[296,128]{1,0:T(8,128)S(1)} %get-tuple-element.12), channel_id=1, source_target_pairs={{0,128},{64,192},{128,0},{192,64},{1,129},{65,193},{129,1},{193,65... | collective-permute-start | bytes 454664 | tf_op jit(solution)/shard_map/ppermute | solution.py:195
  46.3 8.3 %collective-permute-start.5 = (f32[296,128]{1,0:T(8,128)S(1)}, f32[296,128]{1,0:T(8,128)S(1)}, u32[]{:S(2)}, u32[]{:S(2)}) collective-permute-start(f32[296,128]{1,0:T(8,128)S(1)} %get-tuple-element.13), channel_id=1, source_target_pairs={{0,192},{64,0},{128,64},{192,128},{1,193},{65,1},{129,65},{193,129... | collective-permute-start | bytes 454664 | tf_op jit(solution)/shard_map/ppermute | solution.py:195
  48.9 7.3 %collective-permute-start.4 = (f32[296,128]{1,0:T(8,128)S(1)}, f32[296,128]{1,0:T(8,128)S(1)}, u32[]{:S(2)}, u32[]{:S(2)}) collective-permute-start(f32[296,128]{1,0:T(8,128)S(1)} %get-tuple-element.14), channel_id=1, source_target_pairs={{0,64},{64,128},{128,192},{192,0},{1,65},{65,129},{129,193},{193,1... | collective-permute-start | bytes 454664 | tf_op jit(solution)/shard_map/ppermute | solution.py:195
  56.4 11.3 %collective-permute-start.6 = (f32[80,128]{1,0:T(8,128)S(1)}, f32[80,128]{1,0:T(8,128)S(1)}, u32[]{:S(2)}, u32[]{:S(2)}) collective-permute-start(f32[80,128]{1,0:T(8,128)S(1)} %get-tuple-element.17), channel_id=1, source_target_pairs={{0,16},{8,24},{16,0},{24,8},{1,17},{9,25},{17,1},{25,9},{2,18},{10... | collective-permute-start | bytes 122888 | tf_op jit(solution)/shard_map/ppermute | solution.py:195
  65.0 4.1 %collective-permute-start.7 = (f32[80,128]{1,0:T(8,128)S(1)}, f32[80,128]{1,0:T(8,128)S(1)}, u32[]{:S(2)}, u32[]{:S(2)}) collective-permute-start(f32[80,128]{1,0:T(8,128)S(1)} %get-tuple-element.18), channel_id=1, source_target_pairs={{0,8},{8,16},{16,24},{24,0},{1,9},{9,17},{17,25},{25,1},{2,10},{10... | collective-permute-start | bytes 122888 | tf_op jit(solution)/shard_map/ppermute | solution.py:195
  65.7 3.4 %collective-permute-start.8 = (f32[80,128]{1,0:T(8,128)S(1)}, f32[80,128]{1,0:T(8,128)S(1)}, u32[]{:S(2)}, u32[]{:S(2)}) collective-permute-start(f32[80,128]{1,0:T(8,128)S(1)} %get-tuple-element.19), channel_id=1, source_target_pairs={{0,24},{8,0},{16,8},{24,16},{1,25},{9,1},{17,9},{25,17},{2,26},{10... | collective-permute-start | bytes 122888 | tf_op jit(solution)/shard_map/ppermute | solution.py:195
  69.8 13.3 %all-to-all-start.2 = ((f32[8,80,128]{2,1,0:T(8,128)}), f32[8,80,128]{2,1,0:T(8,128)S(1)}, u32[]{:S(2)}, u32[]{:S(2)}) async-start(f32[8,80,128]{2,1,0:T(8,128)} %broadcast_in_dim.21), calls=%async_computation.2 | async-start | bytes 655360 | tf_op jit(solution)/shard_map/all_to_all | solution.py:225
  83.2 4.7 %collective-permute-start.9 = (f32[80,128]{1,0:T(8,128)S(1)}, f32[80,128]{1,0:T(8,128)S(1)}, u32[]{:S(2)}, u32[]{:S(2)}) collective-permute-start(f32[80,128]{1,0:T(8,128)S(1)} %get-tuple-element.20), channel_id=1, source_target_pairs={{0,8},{8,16},{16,24},{24,0},{1,9},{9,17},{17,25},{25,1},{2,10},{10... | collective-permute-start | bytes 122888 | tf_op jit(solution)/shard_map/ppermute | solution.py:206
  83.4 5.9 %collective-permute-start.10 = (f32[80,128]{1,0:T(8,128)S(1)}, f32[80,128]{1,0:T(8,128)S(1)}, u32[]{:S(2)}, u32[]{:S(2)}) collective-permute-start(f32[80,128]{1,0:T(8,128)S(1)} %get-tuple-element.20), channel_id=1, source_target_pairs={{0,16},{8,24},{16,0},{24,8},{1,17},{9,25},{17,1},{25,9},{2,18},{10... | collective-permute-start | bytes 122888 | tf_op jit(solution)/shard_map/ppermute | solution.py:206
  87.5 2.9 %collective-permute-start.11 = (f32[80,128]{1,0:T(8,128)S(1)}, f32[80,128]{1,0:T(8,128)S(1)}, u32[]{:S(2)}, u32[]{:S(2)}) collective-permute-start(f32[80,128]{1,0:T(8,128)S(1)} %get-tuple-element.20), channel_id=1, source_target_pairs={{0,24},{8,0},{16,8},{24,16},{1,25},{9,1},{17,9},{25,17},{2,26},{10... | collective-permute-start | bytes 122888 | tf_op jit(solution)/shard_map/ppermute | solution.py:206
  90.4 5.3 %collective-permute-start.12 = (f32[296,128]{1,0:T(8,128)S(1)}, f32[296,128]{1,0:T(8,128)S(1)}, u32[]{:S(2)}, u32[]{:S(2)}) collective-permute-start(f32[296,128]{1,0:T(8,128)S(1)} %get-tuple-element.15), channel_id=1, source_target_pairs={{0,64},{64,128},{128,192},{192,0},{1,65},{65,129},{129,193},{193,1... | collective-permute-start | bytes 454664 | tf_op jit(solution)/shard_map/ppermute | solution.py:206
  90.5 7.1 %collective-permute-start.13 = (f32[296,128]{1,0:T(8,128)S(1)}, f32[296,128]{1,0:T(8,128)S(1)}, u32[]{:S(2)}, u32[]{:S(2)}) collective-permute-start(f32[296,128]{1,0:T(8,128)S(1)} %get-tuple-element.15), channel_id=1, source_target_pairs={{0,128},{64,192},{128,0},{192,64},{1,129},{65,193},{129,1},{193,65... | collective-permute-start | bytes 454664 | tf_op jit(solution)/shard_map/ppermute | solution.py:206
  93.4 4.6 %collective-permute-start.14 = (f32[296,128]{1,0:T(8,128)S(1)}, f32[296,128]{1,0:T(8,128)S(1)}, u32[]{:S(2)}, u32[]{:S(2)}) collective-permute-start(f32[296,128]{1,0:T(8,128)S(1)} %get-tuple-element.15), channel_id=1, source_target_pairs={{0,192},{64,0},{128,64},{192,128},{1,193},{65,1},{129,65},{193,129... | collective-permute-start | bytes 454664 | tf_op jit(solution)/shard_map/ppermute | solution.py:206
  98.0 9.1 %collective-permute-start.15 = (f32[1184,128]{1,0:T(8,128)S(1)}, f32[1184,128]{1,0:T(8,128)S(1)}, u32[]{:S(2)}, u32[]{:S(2)}) collective-permute-start(f32[1184,128]{1,0:T(8,128)S(1)} %constant_dynamic-update-slice_fusion.2), channel_id=1, source_target_pairs={{0,32},{32,0},{1,33},{33,1},{2,34},{34,2},{3,35},{35,3},{4,36},{36... | collective-permute-start | bytes 1818632 | tf_op jit(solution)/shard_map/ppermute | solution.py:179

commit v4 on v3

--- a/solution.py
+++ b/solution.py
@@ -82,7 +82,7 @@
         place(buf, 32 + s, dxv - rest[1, s])
         return carry
 
-    lax.fori_loop(0, 32, one, 0, unroll=4)
+    lax.fori_loop(0, 32, one, 0, unroll=8)
     emit(buf, out, 64)
 
 

time: 131 us -> 131 us (level)
  no operation moved by 1% of the time
where the time goes in v4:
time: 131 us
  starting transfers between devices  51.3 us (39%)
  waiting for transfers between devices  43.8 us (33%)
  Pallas kernels  30.7 us (23%)
  local copies, waits for them, and re-layouts  3.51 us (3%)
    pallas_call x1, Pallas kernels, chol_solve(): pl.pallas_call(chol_kernel, out_shape=(jax.ShapeDtypeStruct((768, 768), j...  23.2 us
    ppermute x6, starting transfers between devices, scatter_ring(): got.append(lax.ppermute(send, axis, ring(4, k)))  14.1 us
    all_to_all x1, waiting for transfers between devices, body(): lax.all_to_all(outer(velocity, lo, hi, rest), ('x', 'c'), 0, 0, tiled=True)  10.8 us
    all_to_all x1, waiting for transfers between devices, total_of(): lax.all_to_all(jnp.broadcast_to(share[None], (8,) + share.shape), 'z', 0,...  9.86 us
    ppermute x6, waiting for transfers between devices, scatter_ring(): got.append(lax.ppermute(send, axis, ring(4, k)))  8.71 us
    ppermute x6, starting transfers between devices, gather_ring(): parts[k] = lax.ppermute(v, axis, ring(4, k))  7.57 us
    ppermute x1, starting transfers between devices, gather_core(): o = lax.ppermute(v, 'c', SWAP)  7.39 us
    ppermute x6, waiting for transfers between devices, gather_ring(): parts[k] = lax.ppermute(v, axis, ring(4, k))  6.94 us
  transfers between devices with their start and end apart: 19, of which 14 were waited for; matrix products, arithmetic and copies ran while one was open for 0% of the time, Pallas kernels for 5%

profile of v4, /device:TPU:1, one launch (start us, length us, event | category | flops | bytes accessed | tf_op | source)
XLA Modules:
  0.0 130.5 jit_solution(10505765096164804838)
XLA Ops:
  0.6 0.0 copy-start
  0.6 2.3 %fusion.3 = (bf16[32,2,4,8,128]{4,3,2,1,0:T(8,128)(2,1)}, bf16[32,2,4,8,128]{4,3,2,1,0:T(8,128)(2,1)}) fusion(bf16[32,3,5,8,128]{4,3,2,1,0:T(8,128)(2,1)} %vel.3), kind=kLoop, calls=%fused_computation.24 | loop fusion | bytes 2097152 | tf_op jit(solution)/shard_map/slice | solution.py:366
  3.0 1.3 collective-permute-start.1
  4.3 5.8 %collective-permute-start = (bf16[32,2,4,8,128]{4,3,2,1,0:T(8,128)(2,1)}, bf16[32,2,4,8,128]{4,3,2,1,0:T(8,128)(2,1)}, u32[]{:S(2)}, u32[]{:S(2)}) collective-permute-start(bf16[32,2,4,8,128]{4,3,2,1,0:T(8,128)(2,1)} %get-tuple-element.11), channel_id=1, source_target_pairs={{0,1},{1,2},{2,3},{3,4},{4,5},{5,6},{6,7},{7,8},{8,9},{9,10},{10,1... | collective-permute-start | bytes 1572872 | tf_op jit(solution)/shard_map/ppermute | solution.py:365
  10.1 0.0 copy-done
  10.1 3.4 %shard_map.30 = (bf16[8,32,640]{2,1,0:T(8,128)(2,1)}, f32[2,32,5,8,128]{4,3,2,1,0:T(8,128)S(1)}) custom-call(bf16[32,3,5,8,128]{4,3,2,1,0:T(8,128)(2,1)S(1)} %copy-done), custom_call_target="tpu_custom_call" | custom-call | flops 10000000 | bytes 12000000 | tf_op jit(solution)/shard_map/pallas_call | solution.py:90
  13.5 6.1 %all-to-all-start = ((bf16[8,32,640]{2,1,0:T(8,128)(2,1)}), bf16[8,32,640]{2,1,0:T(8,128)(2,1)S(1)}, u32[]{:S(2)}, u32[]{:S(2)}) async-start(bf16[8,32,640]{2,1,0:T(8,128)(2,1)} %get-tuple-element.6), calls=%async_computation | async-start | bytes 655360 | tf_op jit(solution)/shard_map/all_to_all | solution.py:368
  19.6 0.0 collective-permute-done.1.hi
  19.6 0.0 collective-permute-done.lo
  19.6 2.8 %shard_map.31 = bf16[8,64,640]{2,1,0:T(8,128)(2,1)} custom-call(bf16[32,3,5,8,128]{4,3,2,1,0:T(8,128)(2,1)S(1)} %copy-done, bf16[32,2,4,8,128]{4,3,2,1,0:T(8,128)(2,1)} %collective-permute-done.lo, bf16[32,2,4,8,128]{4,3,2,1,0:T(8,128)(2,1)S(1)} %collective-permute-done.1.hi, f32[2,32,5,8,128]{4,3,2,1,0:T(8,128)S(1)} %get-tuple-element.7.rest), custom_call_target="tpu_custom_call" | custom-call | flops 10000000 | bytes 6000000 | tf_op jit(solution)/shard_map/pallas_call | solution.py:102
  22.3 4.3 %all-to-all-done.one = bf16[8,32,640]{2,1,0:T(8,128)(2,1)S(1)} async-done(((bf16[8,32,640]{2,1,0:T(8,128)(2,1)}), bf16[8,32,640]{2,1,0:T(8,128)(2,1)S(1)}, u32[]{:S(2)}, u32[]{:S(2)}) %all-to-all-start) | async-done | bytes 327712 | tf_op jit(solution)/shard_map/all_to_all | solution.py:368
  26.7 4.6 %all-to-all-start.1 = ((bf16[8,64,640]{2,1,0:T(8,128)(2,1)}), bf16[8,64,640]{2,1,0:T(8,128)(2,1)S(1)}, u32[]{:S(2)}, u32[]{:S(2)}) async-start(bf16[8,64,640]{2,1,0:T(8,128)(2,1)} %shard_map.31), calls=%async_computation.1 | async-start | bytes 1310720 | tf_op jit(solution)/shard_map/all_to_all | solution.py:369
  31.2 10.8 %all-to-all-done.1.two = bf16[8,64,640]{2,1,0:T(8,128)(2,1)S(1)} async-done(((bf16[8,64,640]{2,1,0:T(8,128)(2,1)}), bf16[8,64,640]{2,1,0:T(8,128)(2,1)S(1)}, u32[]{:S(2)}, u32[]{:S(2)}) %all-to-all-start.1) | async-done | bytes 655392 | tf_op jit(solution)/shard_map/all_to_all | solution.py:369
  42.0 1.3 shard_map.32
  43.3 1.1 collective-permute-start.2
  44.4 1.7 %collective-permute-done.2 = f32[1184,128]{1,0:T(8,128)S(1)} collective-permute-done((f32[1184,128]{1,0:T(8,128)S(1)}, f32[1184,128]{1,0:T(8,128)S(1)}, u32[]{:S(2)}, u32[]{:S(2)}) %collective-permute-start.2) | collective-permute-done | bytes 606240 | tf_op jit(solution)/shard_map/ppermute | solution.py:173
  46.1 0.1 dynamic-slice_add_fusion
  46.2 0.2 collective-permute-start.3
  46.3 2.6 %collective-permute-start.5 = (f32[296,128]{1,0:T(8,128)S(1)}, f32[296,128]{1,0:T(8,128)S(1)}, u32[]{:S(2)}, u32[]{:S(2)}) collective-permute-start(f32[296,128]{1,0:T(8,128)S(1)} %get-tuple-element.13), channel_id=1, source_target_pairs={{0,192},{64,0},{128,64},{192,128},{1,193},{65,1},{129,65},{193,129... | collective-permute-start | bytes 454664 | tf_op jit(solution)/shard_map/ppermute | solution.py:195
  48.9 0.0 collective-permute-start.4
  49.0 3.9 %collective-permute-done.3 = f32[296,128]{1,0:T(8,128)S(1)} collective-permute-done((f32[296,128]{1,0:T(8,128)S(1)}, f32[296,128]{1,0:T(8,128)S(1)}, u32[]{:S(2)}, u32[]{:S(2)}) %collective-permute-start.3) | collective-permute-done | bytes 151584 | tf_op jit(solution)/shard_map/ppermute | solution.py:195
  52.9 1.7 %collective-permute-done.5 = f32[296,128]{1,0:T(8,128)S(1)} collective-permute-done((f32[296,128]{1,0:T(8,128)S(1)}, f32[296,128]{1,0:T(8,128)S(1)}, u32[]{:S(2)}, u32[]{:S(2)}) %collective-permute-start.5) | collective-permute-done | bytes 151584 | tf_op jit(solution)/shard_map/ppermute | solution.py:195
  54.6 1.7 %collective-permute-done.4 = f32[296,128]{1,0:T(8,128)S(1)} collective-permute-done((f32[296,128]{1,0:T(8,128)S(1)}, f32[296,128]{1,0:T(8,128)S(1)}, u32[]{:S(2)}, u32[]{:S(2)}) %collective-permute-start.4) | collective-permute-done | bytes 151584 | tf_op jit(solution)/shard_map/ppermute | solution.py:195
  56.4 8.6 %collective-permute-start.6 = (f32[80,128]{1,0:T(8,128)S(1)}, f32[80,128]{1,0:T(8,128)S(1)}, u32[]{:S(2)}, u32[]{:S(2)}) collective-permute-start(f32[80,128]{1,0:T(8,128)S(1)} %get-tuple-element.17), channel_id=1, source_target_pairs={{0,16},{8,24},{16,0},{24,8},{1,17},{9,25},{17,1},{25,9},{2,18},{10... | collective-permute-start | bytes 122888 | tf_op jit(solution)/shard_map/ppermute | solution.py:195
  65.0 0.7 collective-permute-start.7
  65.7 2.0 %collective-permute-start.8 = (f32[80,128]{1,0:T(8,128)S(1)}, f32[80,128]{1,0:T(8,128)S(1)}, u32[]{:S(2)}, u32[]{:S(2)}) collective-permute-start(f32[80,128]{1,0:T(8,128)S(1)} %get-tuple-element.19), channel_id=1, source_target_pairs={{0,24},{8,0},{16,8},{24,16},{1,25},{9,1},{17,9},{25,17},{2,26},{10... | collective-permute-start | bytes 122888 | tf_op jit(solution)/shard_map/ppermute | solution.py:195
  67.7 0.0 collective-permute-done.6
  67.7 1.4 %collective-permute-done.7 = f32[80,128]{1,0:T(8,128)S(1)} collective-permute-done((f32[80,128]{1,0:T(8,128)S(1)}, f32[80,128]{1,0:T(8,128)S(1)}, u32[]{:S(2)}, u32[]{:S(2)}) %collective-permute-start.7) | collective-permute-done | bytes 40992 | tf_op jit(solution)/shard_map/ppermute | solution.py:195
  69.1 0.0 collective-permute-done.8
  69.1 0.7 broadcast_in_dim.21
  69.8 3.4 %all-to-all-start.2 = ((f32[8,80,128]{2,1,0:T(8,128)}), f32[8,80,128]{2,1,0:T(8,128)S(1)}, u32[]{:S(2)}, u32[]{:S(2)}) async-start(f32[8,80,128]{2,1,0:T(8,128)} %broadcast_in_dim.21), calls=%async_computation.2 | async-start | bytes 655360 | tf_op jit(solution)/shard_map/all_to_all | solution.py:225
  73.3 9.9 %all-to-all-done.2 = f32[8,80,128]{2,1,0:T(8,128)S(1)} async-done(((f32[8,80,128]{2,1,0:T(8,128)}), f32[8,80,128]{2,1,0:T(8,128)S(1)}, u32[]{:S(2)}, u32[]{:S(2)}) %all-to-all-start.2) | async-done | bytes 327712 | tf_op jit(solution)/shard_map/all_to_all | solution.py:225
  83.2 0.1 collective-permute-start.9
  83.4 4.1 %collective-permute-start.10 = (f32[80,128]{1,0:T(8,128)S(1)}, f32[80,128]{1,0:T(8,128)S(1)}, u32[]{:S(2)}, u32[]{:S(2)}) collective-permute-start(f32[80,128]{1,0:T(8,128)S(1)} %get-tuple-element.20), channel_id=1, source_target_pairs={{0,16},{8,24},{16,0},{24,8},{1,17},{9,25},{17,1},{25,9},{2,18},{10... | collective-permute-start | bytes 122888 | tf_op jit(solution)/shard_map/ppermute | solution.py:206
  87.4 0.4 collective-permute-start.11
  87.9 0.0 collective-permute-done.9
  87.9 1.4 %collective-permute-done.10 = f32[80,128]{1,0:T(8,128)S(1)} collective-permute-done((f32[80,128]{1,0:T(8,128)S(1)}, f32[80,128]{1,0:T(8,128)S(1)}, u32[]{:S(2)}, u32[]{:S(2)}) %collective-permute-start.10) | collective-permute-done | bytes 40992 | tf_op jit(solution)/shard_map/ppermute | solution.py:206
  89.3 1.0 collective-permute-done.11
  90.4 0.1 collective-permute-start.12
  90.5 2.9 %collective-permute-start.13 = (f32[296,128]{1,0:T(8,128)S(1)}, f32[296,128]{1,0:T(8,128)S(1)}, u32[]{:S(2)}, u32[]{:S(2)}) collective-permute-start(f32[296,128]{1,0:T(8,128)S(1)} %get-tuple-element.15), channel_id=1, source_target_pairs={{0,128},{64,192},{128,0},{192,64},{1,129},{65,193},{129,1},{193,65... | collective-permute-start | bytes 454664 | tf_op jit(solution)/shard_map/ppermute | solution.py:206
  93.4 0.0 collective-permute-start.14
  93.4 2.3 %collective-permute-done.12 = f32[296,128]{1,0:T(8,128)S(1)} collective-permute-done((f32[296,128]{1,0:T(8,128)S(1)}, f32[296,128]{1,0:T(8,128)S(1)}, u32[]{:S(2)}, u32[]{:S(2)}) %collective-permute-start.12) | collective-permute-done | bytes 151584 | tf_op jit(solution)/shard_map/ppermute | solution.py:206
  95.7 1.8 %collective-permute-done.13 = f32[296,128]{1,0:T(8,128)S(1)} collective-permute-done((f32[296,128]{1,0:T(8,128)S(1)}, f32[296,128]{1,0:T(8,128)S(1)}, u32[]{:S(2)}, u32[]{:S(2)}) %collective-permute-start.13) | collective-permute-done | bytes 151584 | tf_op jit(solution)/shard_map/ppermute | solution.py:206
  97.6 0.4 collective-permute-done.14
  98.0 7.4 %collective-permute-start.15 = (f32[1184,128]{1,0:T(8,128)S(1)}, f32[1184,128]{1,0:T(8,128)S(1)}, u32[]{:S(2)}, u32[]{:S(2)}) collective-permute-start(f32[1184,128]{1,0:T(8,128)S(1)} %constant_dynamic-update-slice_fusion.2), channel_id=1, source_target_pairs={{0,32},{32,0},{1,33},{33,1},{2,34},{34,2},{3,35},{35,3},{4,36},{36... | collective-permute-start | bytes 1818632 | tf_op jit(solution)/shard_map/ppermute | solution.py:179
  105.4 0.1 broadcast_in_dim.18
  105.5 1.5 %collective-permute-done.15 = f32[1184,128]{1,0:T(8,128)S(1)} collective-permute-done((f32[1184,128]{1,0:T(8,128)S(1)}, f32[1184,128]{1,0:T(8,128)S(1)}, u32[]{:S(2)}, u32[]{:S(2)}) %collective-permute-start.15) | collective-permute-done | bytes 606240 | tf_op jit(solution)/shard_map/ppermute | solution.py:179
  107.1 23.2 %shard_map.33 = (f32[768,768]{1,0:T(8,128)}, bf16[768,640]{1,0:T(8,128)(2,1)}) custom-call(f32[2368,128]{1,0:T(8,128)S(1)} %constant_dynamic-update-slice_fusion.a_ref, bf16[8,32,640]{2,1,0:T(8,128)(2,1)S(1)} %all-to-all-done.one, bf16[8,64,640]{2,1,0:T(8,128)(2,1)S(1)} %all-to-all-done.1.two, f32[8,128]{1,0:T(8,128)S(1)} %broadcast_in_dim.22.ones), custom_call_target="tpu_custom_call" | custom-call | tf_op jit(solution)/shard_map/pallas_call | solution.py:355
  (19 shorter events, 0.4 us)
Async XLA Ops:
  0.6 9.4 %copy-start = (bf16[32,3,5,8,128]{4,3,2,1,0:T(8,128)(2,1)S(1)}, bf16[32,3,5,8,128]{4,3,2,1,0:T(8,128)(2,1)}, u32[]{:S(2)}) copy-start(bf16[32,3,5,8,128]{4,3,2,1,0:T(8,128)(2,1)} %vel.3) | copy-start | bytes 2949124
  3.0 16.6 %collective-permute-start.1 = (bf16[32,2,4,8,128]{4,3,2,1,0:T(8,128)(2,1)}, bf16[32,2,4,8,128]{4,3,2,1,0:T(8,128)(2,1)S(1)}, u32[]{:S(2)}, u32[]{:S(2)}) collective-permute-start(bf16[32,2,4,8,128]{4,3,2,1,0:T(8,128)(2,1)} %get-tuple-element.10), channel_id=1, source_target_pairs={{1,0},{2,1},{3,2},{4,3},{5,4},{6,5},{7,6},{8,7},{9,8},{10,9},{11,1... | collective-permute-start | bytes 1572872 | tf_op jit(solution)/shard_map/ppermute | solution.py:366
  4.3 15.3 %collective-permute-start = (bf16[32,2,4,8,128]{4,3,2,1,0:T(8,128)(2,1)}, bf16[32,2,4,8,128]{4,3,2,1,0:T(8,128)(2,1)}, u32[]{:S(2)}, u32[]{:S(2)}) collective-permute-start(bf16[32,2,4,8,128]{4,3,2,1,0:T(8,128)(2,1)} %get-tuple-element.11), channel_id=1, source_target_pairs={{0,1},{1,2},{2,3},{3,4},{4,5},{5,6},{6,7},{7,8},{8,9},{9,10},{10,1... | collective-permute-start | bytes 1572872 | tf_op jit(solution)/shard_map/ppermute | solution.py:365
  13.5 13.2 %all-to-all-start = ((bf16[8,32,640]{2,1,0:T(8,128)(2,1)}), bf16[8,32,640]{2,1,0:T(8,128)(2,1)S(1)}, u32[]{:S(2)}, u32[]{:S(2)}) async-start(bf16[8,32,640]{2,1,0:T(8,128)(2,1)} %get-tuple-element.6), calls=%async_computation | async-start | bytes 655360 | tf_op jit(solution)/shard_map/all_to_all | solution.py:368
  26.7 15.4 %all-to-all-start.1 = ((bf16[8,64,640]{2,1,0:T(8,128)(2,1)}), bf16[8,64,640]{2,1,0:T(8,128)(2,1)S(1)}, u32[]{:S(2)}, u32[]{:S(2)}) async-start(bf16[8,64,640]{2,1,0:T(8,128)(2,1)} %shard_map.31), calls=%async_computation.1 | async-start | bytes 1310720 | tf_op jit(solution)/shard_map/all_to_all | solution.py:369
  43.3 2.7 %collective-permute-start.2 = (f32[1184,128]{1,0:T(8,128)S(1)}, f32[1184,128]{1,0:T(8,128)S(1)}, u32[]{:S(2)}, u32[]{:S(2)}) collective-permute-start(f32[1184,128]{1,0:T(8,128)S(1)} %constant_dynamic-slice_fusion.3), channel_id=1, source_target_pairs={{0,32},{32,0},{1,33},{33,1},{2,34},{34,2},{3,35},{35,3},{4,36},{36... | collective-permute-start | bytes 1818632 | tf_op jit(solution)/shard_map/ppermute | solution.py:173
  46.2 6.7 %collective-permute-start.3 = (f32[296,128]{1,0:T(8,128)S(1)}, f32[296,128]{1,0:T(8,128)S(1)}, u32[]{:S(2)}, u32[]{:S(2)}) collective-permute-start(f32[296,128]{1,0:T(8,128)S(1)} %get-tuple-element.12), channel_id=1, source_target_pairs={{0,128},{64,192},{128,0},{192,64},{1,129},{65,193},{129,1},{193,65... | collective-permute-start | bytes 454664 | tf_op jit(solution)/shard_map/ppermute | solution.py:195
  46.3 8.3 %collective-permute-start.5 = (f32[296,128]{1,0:T(8,128)S(1)}, f32[296,128]{1,0:T(8,128)S(1)}, u32[]{:S(2)}, u32[]{:S(2)}) collective-permute-start(f32[296,128]{1,0:T(8,128)S(1)} %get-tuple-element.13), channel_id=1, source_target_pairs={{0,192},{64,0},{128,64},{192,128},{1,193},{65,1},{129,65},{193,129... | collective-permute-start | bytes 454664 | tf_op jit(solution)/shard_map/ppermute | solution.py:195
  48.9 7.3 %collective-permute-start.4 = (f32[296,128]{1,0:T(8,128)S(1)}, f32[296,128]{1,0:T(8,128)S(1)}, u32[]{:S(2)}, u32[]{:S(2)}) collective-permute-start(f32[296,128]{1,0:T(8,128)S(1)} %get-tuple-element.14), channel_id=1, source_target_pairs={{0,64},{64,128},{128,192},{192,0},{1,65},{65,129},{129,193},{193,1... | collective-permute-start | bytes 454664 | tf_op jit(solution)/shard_map/ppermute | solution.py:195
  56.4 11.3 %collective-permute-start.6 = (f32[80,128]{1,0:T(8,128)S(1)}, f32[80,128]{1,0:T(8,128)S(1)}, u32[]{:S(2)}, u32[]{:S(2)}) collective-permute-start(f32[80,128]{1,0:T(8,128)S(1)} %get-tuple-element.17), channel_id=1, source_target_pairs={{0,16},{8,24},{16,0},{24,8},{1,17},{9,25},{17,1},{25,9},{2,18},{10... | collective-permute-start | bytes 122888 | tf_op jit(solution)/shard_map/ppermute | solution.py:195
  65.0 4.1 %collective-permute-start.7 = (f32[80,128]{1,0:T(8,128)S(1)}, f32[80,128]{1,0:T(8,128)S(1)}, u32[]{:S(2)}, u32[]{:S(2)}) collective-permute-start(f32[80,128]{1,0:T(8,128)S(1)} %get-tuple-element.18), channel_id=1, source_target_pairs={{0,8},{8,16},{16,24},{24,0},{1,9},{9,17},{17,25},{25,1},{2,10},{10... | collective-permute-start | bytes 122888 | tf_op jit(solution)/shard_map/ppermute | solution.py:195
  65.7 3.4 %collective-permute-start.8 = (f32[80,128]{1,0:T(8,128)S(1)}, f32[80,128]{1,0:T(8,128)S(1)}, u32[]{:S(2)}, u32[]{:S(2)}) collective-permute-start(f32[80,128]{1,0:T(8,128)S(1)} %get-tuple-element.19), channel_id=1, source_target_pairs={{0,24},{8,0},{16,8},{24,16},{1,25},{9,1},{17,9},{25,17},{2,26},{10... | collective-permute-start | bytes 122888 | tf_op jit(solution)/shard_map/ppermute | solution.py:195
  69.8 13.3 %all-to-all-start.2 = ((f32[8,80,128]{2,1,0:T(8,128)}), f32[8,80,128]{2,1,0:T(8,128)S(1)}, u32[]{:S(2)}, u32[]{:S(2)}) async-start(f32[8,80,128]{2,1,0:T(8,128)} %broadcast_in_dim.21), calls=%async_computation.2 | async-start | bytes 655360 | tf_op jit(solution)/shard_map/all_to_all | solution.py:225
  83.2 4.7 %collective-permute-start.9 = (f32[80,128]{1,0:T(8,128)S(1)}, f32[80,128]{1,0:T(8,128)S(1)}, u32[]{:S(2)}, u32[]{:S(2)}) collective-permute-start(f32[80,128]{1,0:T(8,128)S(1)} %get-tuple-element.20), channel_id=1, source_target_pairs={{0,8},{8,16},{16,24},{24,0},{1,9},{9,17},{17,25},{25,1},{2,10},{10... | collective-permute-start | bytes 122888 | tf_op jit(solution)/shard_map/ppermute | solution.py:206
  83.4 5.9 %collective-permute-start.10 = (f32[80,128]{1,0:T(8,128)S(1)}, f32[80,128]{1,0:T(8,128)S(1)}, u32[]{:S(2)}, u32[]{:S(2)}) collective-permute-start(f32[80,128]{1,0:T(8,128)S(1)} %get-tuple-element.20), channel_id=1, source_target_pairs={{0,16},{8,24},{16,0},{24,8},{1,17},{9,25},{17,1},{25,9},{2,18},{10... | collective-permute-start | bytes 122888 | tf_op jit(solution)/shard_map/ppermute | solution.py:206
  87.4 2.9 %collective-permute-start.11 = (f32[80,128]{1,0:T(8,128)S(1)}, f32[80,128]{1,0:T(8,128)S(1)}, u32[]{:S(2)}, u32[]{:S(2)}) collective-permute-start(f32[80,128]{1,0:T(8,128)S(1)} %get-tuple-element.20), channel_id=1, source_target_pairs={{0,24},{8,0},{16,8},{24,16},{1,25},{9,1},{17,9},{25,17},{2,26},{10... | collective-permute-start | bytes 122888 | tf_op jit(solution)/shard_map/ppermute | solution.py:206
  90.4 5.3 %collective-permute-start.12 = (f32[296,128]{1,0:T(8,128)S(1)}, f32[296,128]{1,0:T(8,128)S(1)}, u32[]{:S(2)}, u32[]{:S(2)}) collective-permute-start(f32[296,128]{1,0:T(8,128)S(1)} %get-tuple-element.15), channel_id=1, source_target_pairs={{0,64},{64,128},{128,192},{192,0},{1,65},{65,129},{129,193},{193,1... | collective-permute-start | bytes 454664 | tf_op jit(solution)/shard_map/ppermute | solution.py:206
  90.5 7.1 %collective-permute-start.13 = (f32[296,128]{1,0:T(8,128)S(1)}, f32[296,128]{1,0:T(8,128)S(1)}, u32[]{:S(2)}, u32[]{:S(2)}) collective-permute-start(f32[296,128]{1,0:T(8,128)S(1)} %get-tuple-element.15), channel_id=1, source_target_pairs={{0,128},{64,192},{128,0},{192,64},{1,129},{65,193},{129,1},{193,65... | collective-permute-start | bytes 454664 | tf_op jit(solution)/shard_map/ppermute | solution.py:206
  93.4 4.6 %collective-permute-start.14 = (f32[296,128]{1,0:T(8,128)S(1)}, f32[296,128]{1,0:T(8,128)S(1)}, u32[]{:S(2)}, u32[]{:S(2)}) collective-permute-start(f32[296,128]{1,0:T(8,128)S(1)} %get-tuple-element.15), channel_id=1, source_target_pairs={{0,192},{64,0},{128,64},{192,128},{1,193},{65,1},{129,65},{193,129... | collective-permute-start | bytes 454664 | tf_op jit(solution)/shard_map/ppermute | solution.py:206
  98.0 9.0 %collective-permute-start.15 = (f32[1184,128]{1,0:T(8,128)S(1)}, f32[1184,128]{1,0:T(8,128)S(1)}, u32[]{:S(2)}, u32[]{:S(2)}) collective-permute-start(f32[1184,128]{1,0:T(8,128)S(1)} %constant_dynamic-update-slice_fusion.2), channel_id=1, source_target_pairs={{0,32},{32,0},{1,33},{33,1},{2,34},{34,2},{3,35},{35,3},{4,36},{36... | collective-permute-start | bytes 1818632 | tf_op jit(solution)/shard_map/ppermute | solution.py:179
